TPU v7x, 128 devices: a whole 4x4x4 slice. The times are simulated.
128 devices in a mesh: gx: 16 (over y, z), yz: 8 (over x, core).
Axes of the slice: x: 4, y: 4, z: 4, core: 2. Of those that a mesh axis runs over, the one named last changes fastest.
Arguments:
- right_side: float32 [64, 256, 512], P('gx', 'yz'), may hold values from -5 to 5
- phase: int32 [64, 256, 512], P('gx', 'yz'), may hold values 0 or 1
- pressure_guess: float32 [64, 256, 512], P('gx', 'yz'), may hold values from -6 to 6
Outputs:
- pressure: float32 [64, 256, 512], P('gx', 'yz')
- residual: float32 [64, 256, 512], P('gx', 'yz')
All inputs are finite; a program needn't handle non-finite values. No bound on the sum of `phase` on one device may be relied on, other than what follows from the above.
Results may differ from a plain program's by a relative error of at most 0.0003.
Values sent between devices are 32-bit elements; how exact they have to be, the bound alone decides.
A program may use at most 128 MiB of HBM per device.

v0:
```python
import jax
import jax.numpy as jnp
from jax import lax
from jax.sharding import PartitionSpec as P

SWEEPS = 2
BOTTOM_SWEEPS = 4


def with_halo(x, sides, width):
    for axis, dim in sides:
        size, length = (lax.axis_size(axis), x.shape[dim])
        up = [(i, (i + 1) % size) for i in range(size - 1)]
        down = [(j, i) for i, j in up]
        last = lax.slice_in_dim(x, length - width, length, axis=dim)
        first = lax.slice_in_dim(x, 0, width, axis=dim)
        before = lax.ppermute(last, axis, up)
        after = lax.ppermute(first, axis, down)
        x = jnp.concatenate([before, x, after], axis=dim)
    return x


def harmonic(left, right):
    total = left + right
    safe = jnp.where(total > 0, total, 1.0)
    return jnp.where(total > 0, 2.0 * left * right / safe, 0.0)


def coefficients(padded):
    faces_x = harmonic(padded[1:], padded[:-1])
    faces_y = harmonic(padded[:, 1:], padded[:, :-1])
    centre = padded[1:-1, 1:-1]
    faces_z = harmonic(centre[:, :, 1:], centre[:, :, :-1])
    zero_plane = jnp.zeros_like(centre[:, :, :1])
    x_lower = faces_x[:-1, 1:-1]
    x_upper = faces_x[1:, 1:-1]
    y_lower = faces_y[1:-1, :-1]
    y_upper = faces_y[1:-1, 1:]
    z_lower = jnp.concatenate([zero_plane, faces_z], axis=2)
    z_upper = jnp.concatenate([faces_z, 2.0 * centre[:, :, -1:]], axis=2)
    diagonal = x_lower + x_upper + y_lower + y_upper + z_lower + z_upper
    diagonal = jnp.where(diagonal > 0, diagonal, 1.0)
    return (x_lower, x_upper, y_lower, y_upper, z_lower, z_upper, diagonal)


def parity_of(extent, start_x, start_y):
    index_x = lax.broadcasted_iota(jnp.int32, extent, 0) + start_x
    index_y = lax.broadcasted_iota(jnp.int32, extent, 1) + start_y
    index_z = lax.broadcasted_iota(jnp.int32, extent, 2)
    return (index_x + index_y + index_z) % 2


def neighbours(padded, coeffs):
    centre = padded[1:-1, 1:-1]
    zero_plane = jnp.zeros_like(centre[:, :, :1])
    lower_z = jnp.concatenate([zero_plane, centre[:, :, :-1]], axis=2)
    upper_z = jnp.concatenate([centre[:, :, 1:], zero_plane], axis=2)
    beside_all = coeffs[0] * padded[:-2, 1:-1] + coeffs[1] * padded[2:, 1:-1]
    beside_all = beside_all + coeffs[2] * padded[1:-1, :-2] + coeffs[3] * padded[1:-1, 2:]
    beside_all = beside_all + coeffs[4] * lower_z + coeffs[5] * upper_z
    return (beside_all, centre)


def colour_pass(padded, source, coeffs, parity, colour):
    beside_all, centre = neighbours(padded, coeffs)
    updated = (source + beside_all) / coeffs[6]
    return jnp.where(parity == colour, updated, centre)


def residual_of(padded, source, coeffs):
    beside_all, centre = neighbours(padded, coeffs)
    return source - (coeffs[6] * centre - beside_all)


def restrict_sum(field):
    size_x, size_y, size_z = field.shape
    return 0.5 * field.reshape(size_x // 2, 2, size_y // 2, 2, size_z // 2, 2).sum(axis=(1, 3, 5))


def restrict_mean(field):
    size_x, size_y, size_z = field.shape
    return 0.125 * field.reshape(size_x // 2, 2, size_y // 2, 2, size_z // 2, 2).sum(axis=(1, 3, 5))


def inject(field):
    return jnp.repeat(jnp.repeat(jnp.repeat(field, 2, axis=0), 2, axis=1), 2, axis=2)


def rim_one(field):
    return with_halo(field, (("gx", 0), ("yz", 1)), 1)


def offsets(field):
    return (lax.axis_index("gx") * field.shape[0], lax.axis_index("yz") * field.shape[1])


def prepare_plain(mobility):
    start_x, start_y = offsets(mobility)
    return (coefficients(rim_one(mobility)), parity_of(mobility.shape, start_x, start_y))


def prepare(mobility):
    operator_set = prepare_plain(mobility)
    return operator_set


def smooth_plain(field, source, operator_set, sweeps, rim):
    coeffs = operator_set[0]
    parity = operator_set[1]
    for _ in range(sweeps):
        field = colour_pass(rim(field), source, coeffs, parity, 0)
        field = colour_pass(rim(field), source, coeffs, parity, 1)
    return field


def smooth(field, source, operator_set, sweeps):
    field = smooth_plain(field, source, operator_set, sweeps, rim_one)
    return field


def local(right_side, phase, pressure_guess):
    mobility = 1.0 + 999.0 * phase.astype(jnp.float32)
    level_zero = prepare(mobility)
    pressure = smooth(pressure_guess, right_side, level_zero, SWEEPS)
    fine_res = residual_of(rim_one(pressure), right_side, level_zero[0])
    source_one = restrict_sum(fine_res)
    mobility_one = restrict_mean(mobility)
    level_one = prepare(mobility_one)
    coarse_one = smooth(jnp.zeros_like(source_one), source_one, level_one, SWEEPS)
    res_one = residual_of(rim_one(coarse_one), source_one, level_one[0])
    source_two = restrict_sum(res_one)
    mobility_two = restrict_mean(mobility_one)
    level_two = prepare_plain(mobility_two)
    coarse_two = smooth_plain(
        jnp.zeros_like(source_two), source_two, level_two, BOTTOM_SWEEPS, rim_one
    )
    coarse_one = smooth(coarse_one + inject(coarse_two), source_one, level_one, SWEEPS)
    pressure = smooth(pressure + inject(coarse_one), right_side, level_zero, SWEEPS)
    residual = residual_of(rim_one(pressure), right_side, level_zero[0])
    return (pressure, residual)


def solution(mesh):
    in_specs = (P("gx", "yz", None), P("gx", "yz", None), P("gx", "yz", None))
    out_specs = (P("gx", "yz", None), P("gx", "yz", None))
    return jax.shard_map(local, mesh=mesh, in_specs=in_specs, out_specs=out_specs, check_vma=False)
```

profile of v0, /device:TPU:97, one launch (start us, length us, event | category | flops | bytes accessed | tf_op | source)
XLA Modules:
  0.0 747.6 jit_solution(1787874520709332939)
XLA Ops:
  2.6 3.4 collective-permute-start.29
  7.6 18.1 %reshape.169 = f32[2,2,16,2,256,2]{5,4,3,2,1,0:T(8,128)} reshape(f32[4,32,512]{2,1,0:T(8,128)S(1)} %copy.203) | data formatting | bytes 524288 | tf_op jit(solution)/shard_map/reshape | solution.py:82
  25.7 7.0 reduce_sum.43
  34.0 4.0 collective-permute-start.48
  40.0 5.6 collective-permute-start
  54.1 3.4 collective-permute-start.25
  60.7 4.8 collective-permute-start.4
  68.2 5.5 collective-permute-start.52
  73.8 6.7 collective-permute-start.2
  85.3 3.6 collective-permute-start.6
  101.3 3.6 collective-permute-start.50
  112.1 3.8 divide_select_fusion
  117.7 5.7 collective-permute-start.8
  130.4 5.3 collective-permute-done.9
  145.1 3.6 collective-permute-start.26
  156.2 5.5 fusion.90
  165.4 3.4 collective-permute-start.13
  177.4 5.4 collective-permute-start.14
  193.3 5.5 fusion.80
  202.5 3.4 collective-permute-start.17
  214.5 4.1 collective-permute-start.18
  229.0 5.5 fusion.70
  238.2 3.4 collective-permute-start.21
  250.2 4.0 collective-permute-start.22
  259.2 3.6 collective-permute-start.30
  270.6 6.4 fusion.60
  278.5 18.1 %reshape.168 = f32[2,2,16,2,256,2]{5,4,3,2,1,0:T(8,128)} reshape(f32[4,32,512]{2,1,0:T(8,128)S(1)} %copy.243) | data formatting | bytes 524288 | tf_op jit(solution)/shard_map/reshape | solution.py:77
  296.6 7.0 reduce_sum.39
  308.4 3.4 collective-permute-start.33
  312.6 4.2 collective-permute-start.54
  330.9 3.5 collective-permute-done.37
  334.4 4.4 collective-permute-start.38
  345.7 3.4 collective-permute-start.41
  362.4 3.4 collective-permute-start.45
  383.4 3.4 collective-permute-start.57
  400.7 3.4 collective-permute-start.61
  417.9 3.4 collective-permute-start.65
  435.2 3.4 collective-permute-start.69
  452.4 3.4 collective-permute-start.73
  469.6 3.4 collective-permute-start.77
  486.9 3.4 collective-permute-start.81
  504.4 3.4 collective-permute-start.85
  521.1 3.4 collective-permute-start.89
  537.8 3.4 collective-permute-start.93
  574.7 3.5 collective-permute-start.101
  582.0 3.6 collective-permute-done.101
  586.7 4.0 collective-permute-start.102
  600.2 5.4 fusion.51
  609.3 3.4 collective-permute-start.105
  616.5 3.6 collective-permute-done.105
  621.3 4.1 collective-permute-start.106
  634.8 5.4 fusion.41
  643.9 3.4 collective-permute-start.109
  651.1 3.6 collective-permute-done.109
  655.9 4.0 collective-permute-start.110
  669.4 5.4 fusion.31
  678.5 3.4 collective-permute-start.113
  685.7 3.6 collective-permute-done.113
  690.5 4.0 collective-permute-start.114
  704.0 5.4 fusion.21
  713.1 3.4 collective-permute-start.117
  720.3 3.6 collective-permute-done.117
  725.1 4.0 collective-permute-start.118
  738.6 6.6 fusion.11
  (498 shorter events, 446.2 us)
Async XLA Ops:
  0.6 117.1 %collective-permute-start.28 = (f32[1,16,256]{2,1,0:T(8,128)S(1)}, f32[1,16,256]{2,1,0:T(8,128)S(1)}, u32[]{:S(2)}, u32[]{:S(2)}) collective-permute-start(f32[1,16,256]{2,1,0:T(8,128)S(1)} %broadcast.338), channel_id=1, source_target_pairs={{0,8},{8,16},{16,24},{24,32},{32,40},{40,48},{48,56},{56,64},{64,7... | collective-permute-start | bytes 49160 | tf_op jit(solution)/shard_map/ppermute | solution.py:17
  2.6 120.9 %collective-permute-start.29 = (f32[1,16,256]{2,1,0:T(8,128)S(1)}, f32[1,16,256]{2,1,0:T(8,128)S(1)}, u32[]{:S(2)}, u32[]{:S(2)}) collective-permute-start(f32[1,16,256]{2,1,0:T(8,128)S(1)} %broadcast.338), channel_id=1, source_target_pairs={{8,0},{16,8},{24,16},{32,24},{40,32},{48,40},{56,48},{64,56},{72,6... | collective-permute-start | bytes 49160 | tf_op jit(solution)/shard_map/ppermute | solution.py:18
  34.0 18.2 %collective-permute-start.48 = (f32[1,8,128]{2,1,0:T(8,128)S(1)}, f32[1,8,128]{2,1,0:T(8,128)S(1)}, u32[]{:S(2)}, u32[]{:S(2)}) collective-permute-start(f32[1,8,128]{2,1,0:T(8,128)S(1)} %multiply_bitcast_fusion), channel_id=1, source_target_pairs={{0,8},{8,16},{16,24},{24,32},{32,40},{40,48},{48,56},{56,64},{64,7... | collective-permute-start | bytes 12296 | tf_op jit(solution)/shard_map/ppermute | solution.py:17
  38.0 16.1 %collective-permute-start.49 = (f32[1,8,128]{2,1,0:T(8,128)S(1)}, f32[1,8,128]{2,1,0:T(8,128)S(1)}, u32[]{:S(2)}, u32[]{:S(2)}) collective-permute-start(f32[1,8,128]{2,1,0:T(8,128)S(1)} %multiply_bitcast_fusion), channel_id=1, source_target_pairs={{8,0},{16,8},{24,16},{32,24},{40,32},{48,40},{56,48},{64,56},{72,6... | collective-permute-start | bytes 12296 | tf_op jit(solution)/shard_map/ppermute | solution.py:18
  40.0 25.5 %collective-permute-start = (f32[1,32,512]{1,2,0:T(8,128)S(1)}, f32[1,32,512]{1,2,0:T(8,128)S(1)}, u32[]{:S(2)}, u32[]{:S(2)}) collective-permute-start(f32[1,32,512]{1,2,0:T(8,128)S(1)} %get-tuple-element.46), channel_id=1, source_target_pairs={{0,8},{8,16},{16,24},{24,32},{32,40},{40,48},{48,56},{56,64},{64,7... | collective-permute-start | bytes 196616 | tf_op jit(solution)/shard_map/ppermute | solution.py:17
  54.1 6.6 collective-permute-start.25
  58.1 9.5 %collective-permute-start.1 = (f32[1,32,512]{1,2,0:T(8,128)S(1)}, f32[1,32,512]{1,2,0:T(8,128)S(1)}, u32[]{:S(2)}, u32[]{:S(2)}) collective-permute-start(f32[1,32,512]{1,2,0:T(8,128)S(1)} %get-tuple-element.47), channel_id=1, source_target_pairs={{8,0},{16,8},{24,16},{32,24},{40,32},{48,40},{56,48},{64,56},{72,6... | collective-permute-start | bytes 196616 | tf_op jit(solution)/shard_map/ppermute | solution.py:18
  60.7 13.1 %collective-permute-start.4 = (f32[1,32,512]{2,1,0:T(8,128)S(1)}, f32[1,32,512]{2,1,0:T(8,128)S(1)}, u32[]{:S(2)}, u32[]{:S(2)}) collective-permute-start(f32[1,32,512]{2,1,0:T(8,128)S(1)} %get-tuple-element.100), channel_id=1, source_target_pairs={{0,8},{8,16},{16,24},{24,32},{32,40},{40,48},{48,56},{56,64},{64,7... | collective-permute-start | bytes 196616 | tf_op jit(solution)/shard_map/ppermute | solution.py:17
  65.5 15.0 %collective-permute-start.5 = (f32[1,32,512]{2,1,0:T(8,128)S(1)}, f32[1,32,512]{2,1,0:T(8,128)S(1)}, u32[]{:S(2)}, u32[]{:S(2)}) collective-permute-start(f32[1,32,512]{2,1,0:T(8,128)S(1)} %get-tuple-element.99), channel_id=1, source_target_pairs={{8,0},{16,8},{24,16},{32,24},{40,32},{48,40},{56,48},{64,56},{72,6... | collective-permute-start | bytes 196616 | tf_op jit(solution)/shard_map/ppermute | solution.py:18
  68.2 240.2 %collective-permute-start.52 = (f32[1,8,128]{2,1,0:T(8,128)}, f32[1,8,128]{2,1,0:T(8,128)}, u32[]{:S(2)}, u32[]{:S(2)}) collective-permute-start(f32[1,8,128]{2,1,0:T(8,128)} %broadcast.344), channel_id=1, source_target_pairs={{0,8},{8,16},{16,24},{24,32},{32,40},{40,48},{48,56},{56,64},{64,7... | collective-permute-start | bytes 12296 | tf_op jit(solution)/shard_map/ppermute | solution.py:17
  73.8 11.5 %collective-permute-start.2 = (f32[6,1,512]{2,1,0:T(1,128)S(1)}, f32[6,1,512]{2,1,0:T(1,128)S(1)}, u32[]{:S(2)}, u32[]{:S(2)}) collective-permute-start(f32[6,1,512]{2,1,0:T(1,128)S(1)} %get-tuple-element.91), channel_id=1, source_target_pairs={{0,1},{1,2},{2,3},{3,4},{4,5},{5,6},{6,7},{8,9},{9,10},{10,11},{11... | collective-permute-start | bytes 36872 | tf_op jit(solution)/shard_map/ppermute | solution.py:17
  80.5 8.4 %collective-permute-start.3 = (f32[6,1,512]{2,1,0:T(1,128)S(1)}, f32[6,1,512]{2,1,0:T(1,128)S(1)}, u32[]{:S(2)}, u32[]{:S(2)}) collective-permute-start(f32[6,1,512]{2,1,0:T(1,128)S(1)} %get-tuple-element.90), channel_id=1, source_target_pairs={{1,0},{2,1},{3,2},{4,3},{5,4},{6,5},{7,6},{9,8},{10,9},{11,10},{12... | collective-permute-start | bytes 36872 | tf_op jit(solution)/shard_map/ppermute | solution.py:18
  85.3 14.1 %collective-permute-start.6 = (f32[6,1,512]{2,1,0:T(1,128)S(1)}, f32[6,1,512]{2,1,0:T(1,128)S(1)}, u32[]{:S(2)}, u32[]{:S(2)}) collective-permute-start(f32[6,1,512]{2,1,0:T(1,128)S(1)} %get-tuple-element.94), channel_id=1, source_target_pairs={{0,1},{1,2},{2,3},{3,4},{4,5},{5,6},{6,7},{8,9},{9,10},{10,11},{11... | collective-permute-start | bytes 36872 | tf_op jit(solution)/shard_map/ppermute | solution.py:17
  88.9 12.3 %collective-permute-start.7 = (f32[6,1,512]{2,1,0:T(1,128)S(1)}, f32[6,1,512]{2,1,0:T(1,128)S(1)}, u32[]{:S(2)}, u32[]{:S(2)}) collective-permute-start(f32[6,1,512]{2,1,0:T(1,128)S(1)} %get-tuple-element.95), channel_id=1, source_target_pairs={{1,0},{2,1},{3,2},{4,3},{5,4},{6,5},{7,6},{9,8},{10,9},{11,10},{12... | collective-permute-start | bytes 36872 | tf_op jit(solution)/shard_map/ppermute | solution.py:18
  99.3 212.5 %collective-permute-start.53 = (f32[1,8,128]{2,1,0:T(8,128)}, f32[1,8,128]{2,1,0:T(8,128)}, u32[]{:S(2)}, u32[]{:S(2)}) collective-permute-start(f32[1,8,128]{2,1,0:T(8,128)} %broadcast.344), channel_id=1, source_target_pairs={{8,0},{16,8},{24,16},{32,24},{40,32},{48,40},{56,48},{64,56},{72,6... | collective-permute-start | bytes 12296 | tf_op jit(solution)/shard_map/ppermute | solution.py:18
  101.3 226.5 %collective-permute-start.50 = (f32[3,1,128]{2,1,0:T(1,128)}, f32[3,1,128]{2,1,0:T(1,128)}, u32[]{:S(2)}, u32[]{:S(2)}) collective-permute-start(f32[3,1,128]{2,1,0:T(1,128)} %get-tuple-element.172), channel_id=1, source_target_pairs={{0,1},{1,2},{2,3},{3,4},{4,5},{5,6},{6,7},{8,9},{9,10},{10,11},{11... | collective-permute-start | bytes 4616 | tf_op jit(solution)/shard_map/ppermute | solution.py:17
  117.7 11.7 %collective-permute-start.8 = (f32[1,32,512]{1,2,0:T(8,128)}, f32[1,32,512]{1,2,0:T(8,128)}, u32[]{:S(2)}, u32[]{:S(2)}) collective-permute-start(f32[1,32,512]{1,2,0:T(8,128)} %get-tuple-element.44), channel_id=1, source_target_pairs={{0,8},{8,16},{16,24},{24,32},{32,40},{40,48},{48,56},{56,64},{64,7... | collective-permute-start | bytes 196616 | tf_op jit(solution)/shard_map/ppermute | solution.py:17
  123.5 12.2 %collective-permute-start.9 = (f32[1,32,512]{1,2,0:T(8,128)}, f32[1,32,512]{1,2,0:T(8,128)}, u32[]{:S(2)}, u32[]{:S(2)}) collective-permute-start(f32[1,32,512]{1,2,0:T(8,128)} %get-tuple-element.45), channel_id=1, source_target_pairs={{8,0},{16,8},{24,16},{32,24},{40,32},{48,40},{56,48},{64,56},{72,6... | collective-permute-start | bytes 196616 | tf_op jit(solution)/shard_map/ppermute | solution.py:18
  136.8 8.3 %collective-permute-start.10 = (f32[6,1,512]{2,1,0:T(1,128)S(1)}, f32[6,1,512]{2,1,0:T(1,128)S(1)}, u32[]{:S(2)}, u32[]{:S(2)}) collective-permute-start(f32[6,1,512]{2,1,0:T(1,128)S(1)} %get-tuple-element.86), channel_id=1, source_target_pairs={{0,1},{1,2},{2,3},{3,4},{4,5},{5,6},{6,7},{8,9},{9,10},{10,11},{11... | collective-permute-start | bytes 36872 | tf_op jit(solution)/shard_map/ppermute | solution.py:17
  139.9 8.9 %collective-permute-start.11 = (f32[6,1,512]{2,1,0:T(1,128)S(1)}, f32[6,1,512]{2,1,0:T(1,128)S(1)}, u32[]{:S(2)}, u32[]{:S(2)}) collective-permute-start(f32[6,1,512]{2,1,0:T(1,128)S(1)} %get-tuple-element.87), channel_id=1, source_target_pairs={{1,0},{2,1},{3,2},{4,3},{5,4},{6,5},{7,6},{9,8},{10,9},{11,10},{12... | collective-permute-start | bytes 36872 | tf_op jit(solution)/shard_map/ppermute | solution.py:18
  145.1 18.3 %collective-permute-start.26 = (f32[4,1,256]{2,1,0:T(1,128)S(1)}, f32[4,1,256]{2,1,0:T(1,128)S(1)}, u32[]{:S(2)}, u32[]{:S(2)}) collective-permute-start(f32[4,1,256]{2,1,0:T(1,128)S(1)} %get-tuple-element.118), channel_id=1, source_target_pairs={{0,1},{1,2},{2,3},{3,4},{4,5},{5,6},{6,7},{8,9},{9,10},{10,11},{11... | collective-permute-start | bytes 12296 | tf_op jit(solution)/shard_map/ppermute | solution.py:17
  148.8 16.6 %collective-permute-start.27 = (f32[4,1,256]{2,1,0:T(1,128)S(1)}, f32[4,1,256]{2,1,0:T(1,128)S(1)}, u32[]{:S(2)}, u32[]{:S(2)}) collective-permute-start(f32[4,1,256]{2,1,0:T(1,128)S(1)} %get-tuple-element.117), channel_id=1, source_target_pairs={{1,0},{2,1},{3,2},{4,3},{5,4},{6,5},{7,6},{9,8},{10,9},{11,10},{12... | collective-permute-start | bytes 12296 | tf_op jit(solution)/shard_map/ppermute | solution.py:18
  163.5 9.1 %collective-permute-start.12 = (f32[1,32,512]{1,2,0:T(8,128)}, f32[1,32,512]{1,2,0:T(8,128)}, u32[]{:S(2)}, u32[]{:S(2)}) collective-permute-start(f32[1,32,512]{1,2,0:T(8,128)} %get-tuple-element.40), channel_id=1, source_target_pairs={{0,8},{8,16},{16,24},{24,32},{32,40},{40,48},{48,56},{56,64},{64,7... | collective-permute-start | bytes 196616 | tf_op jit(solution)/shard_map/ppermute | solution.py:17
  165.4 11.0 %collective-permute-start.13 = (f32[1,32,512]{1,2,0:T(8,128)}, f32[1,32,512]{1,2,0:T(8,128)}, u32[]{:S(2)}, u32[]{:S(2)}) collective-permute-start(f32[1,32,512]{1,2,0:T(8,128)} %get-tuple-element.41), channel_id=1, source_target_pairs={{8,0},{16,8},{24,16},{32,24},{40,32},{48,40},{56,48},{64,56},{72,6... | collective-permute-start | bytes 196616 | tf_op jit(solution)/shard_map/ppermute | solution.py:18
  177.4 10.4 %collective-permute-start.14 = (f32[6,1,512]{2,1,0:T(1,128)S(1)}, f32[6,1,512]{2,1,0:T(1,128)S(1)}, u32[]{:S(2)}, u32[]{:S(2)}) collective-permute-start(f32[6,1,512]{2,1,0:T(1,128)S(1)} %get-tuple-element.82), channel_id=1, source_target_pairs={{0,1},{1,2},{2,3},{3,4},{4,5},{5,6},{6,7},{8,9},{9,10},{10,11},{11... | collective-permute-start | bytes 36872 | tf_op jit(solution)/shard_map/ppermute | solution.py:17
  200.6 9.1 %collective-permute-start.16 = (f32[1,32,512]{1,2,0:T(8,128)}, f32[1,32,512]{1,2,0:T(8,128)}, u32[]{:S(2)}, u32[]{:S(2)}) collective-permute-start(f32[1,32,512]{1,2,0:T(8,128)} %get-tuple-element.36), channel_id=1, source_target_pairs={{0,8},{8,16},{16,24},{24,32},{32,40},{40,48},{48,56},{56,64},{64,7... | collective-permute-start | bytes 196616 | tf_op jit(solution)/shard_map/ppermute | solution.py:17
  202.5 10.9 %collective-permute-start.17 = (f32[1,32,512]{1,2,0:T(8,128)}, f32[1,32,512]{1,2,0:T(8,128)}, u32[]{:S(2)}, u32[]{:S(2)}) collective-permute-start(f32[1,32,512]{1,2,0:T(8,128)} %get-tuple-element.37), channel_id=1, source_target_pairs={{8,0},{16,8},{24,16},{32,24},{40,32},{48,40},{56,48},{64,56},{72,6... | collective-permute-start | bytes 196616 | tf_op jit(solution)/shard_map/ppermute | solution.py:18
  214.5 9.0 %collective-permute-start.18 = (f32[6,1,512]{2,1,0:T(1,128)S(1)}, f32[6,1,512]{2,1,0:T(1,128)S(1)}, u32[]{:S(2)}, u32[]{:S(2)}) collective-permute-start(f32[6,1,512]{2,1,0:T(1,128)S(1)} %get-tuple-element.78), channel_id=1, source_target_pairs={{0,1},{1,2},{2,3},{3,4},{4,5},{5,6},{6,7},{8,9},{9,10},{10,11},{11... | collective-permute-start | bytes 36872 | tf_op jit(solution)/shard_map/ppermute | solution.py:17
  236.3 9.1 %collective-permute-start.20 = (f32[1,32,512]{1,2,0:T(8,128)}, f32[1,32,512]{1,2,0:T(8,128)}, u32[]{:S(2)}, u32[]{:S(2)}) collective-permute-start(f32[1,32,512]{1,2,0:T(8,128)} %get-tuple-element.32), channel_id=1, source_target_pairs={{0,8},{8,16},{16,24},{24,32},{32,40},{40,48},{48,56},{56,64},{64,7... | collective-permute-start | bytes 196616 | tf_op jit(solution)/shard_map/ppermute | solution.py:17
  238.2 10.9 %collective-permute-start.21 = (f32[1,32,512]{1,2,0:T(8,128)}, f32[1,32,512]{1,2,0:T(8,128)}, u32[]{:S(2)}, u32[]{:S(2)}) collective-permute-start(f32[1,32,512]{1,2,0:T(8,128)} %get-tuple-element.33), channel_id=1, source_target_pairs={{8,0},{16,8},{24,16},{32,24},{40,32},{48,40},{56,48},{64,56},{72,6... | collective-permute-start | bytes 196616 | tf_op jit(solution)/shard_map/ppermute | solution.py:18
  250.2 9.0 %collective-permute-start.22 = (f32[6,1,512]{2,1,0:T(1,128)S(1)}, f32[6,1,512]{2,1,0:T(1,128)S(1)}, u32[]{:S(2)}, u32[]{:S(2)}) collective-permute-start(f32[6,1,512]{2,1,0:T(1,128)S(1)} %get-tuple-element.74), channel_id=1, source_target_pairs={{0,1},{1,2},{2,3},{3,4},{4,5},{5,6},{6,7},{8,9},{9,10},{10,11},{11... | collective-permute-start | bytes 36872 | tf_op jit(solution)/shard_map/ppermute | solution.py:17
  254.2 8.6 %collective-permute-start.23 = (f32[6,1,512]{2,1,0:T(1,128)S(1)}, f32[6,1,512]{2,1,0:T(1,128)S(1)}, u32[]{:S(2)}, u32[]{:S(2)}) collective-permute-start(f32[6,1,512]{2,1,0:T(1,128)S(1)} %get-tuple-element.75), channel_id=1, source_target_pairs={{1,0},{2,1},{3,2},{4,3},{5,4},{6,5},{7,6},{9,8},{10,9},{11,10},{12... | collective-permute-start | bytes 36872 | tf_op jit(solution)/shard_map/ppermute | solution.py:18
  259.2 44.5 %collective-permute-start.30 = (f32[4,1,256]{2,1,0:T(1,128)}, f32[4,1,256]{2,1,0:T(1,128)}, u32[]{:S(2)}, u32[]{:S(2)}) collective-permute-start(f32[4,1,256]{2,1,0:T(1,128)} %get-tuple-element.119), channel_id=1, source_target_pairs={{0,1},{1,2},{2,3},{3,4},{4,5},{5,6},{6,7},{8,9},{9,10},{10,11},{11... | collective-permute-start | bytes 12296 | tf_op jit(solution)/shard_map/ppermute | solution.py:17
  262.8 42.8 %collective-permute-start.31 = (f32[4,1,256]{2,1,0:T(1,128)}, f32[4,1,256]{2,1,0:T(1,128)}, u32[]{:S(2)}, u32[]{:S(2)}) collective-permute-start(f32[4,1,256]{2,1,0:T(1,128)} %get-tuple-element.120), channel_id=1, source_target_pairs={{1,0},{2,1},{3,2},{4,3},{5,4},{6,5},{7,6},{9,8},{10,9},{11,10},{12... | collective-permute-start | bytes 12296 | tf_op jit(solution)/shard_map/ppermute | solution.py:18
  303.7 26.5 %collective-permute-start.51 = (f32[3,1,128]{2,1,0:T(1,128)S(1)}, f32[3,1,128]{2,1,0:T(1,128)S(1)}, u32[]{:S(2)}, u32[]{:S(2)}) collective-permute-start(f32[3,1,128]{2,1,0:T(1,128)S(1)} %copy-done.48), channel_id=1, source_target_pairs={{1,0},{2,1},{3,2},{4,3},{5,4},{6,5},{7,6},{9,8},{10,9},{11,10},{12... | collective-permute-start | bytes 4616 | tf_op jit(solution)/shard_map/ppermute | solution.py:18
  306.5 10.3 %collective-permute-start.32 = (f32[1,16,256]{2,1,0:T(8,128)S(1)}, f32[1,16,256]{2,1,0:T(8,128)S(1)}, u32[]{:S(2)}, u32[]{:S(2)}) collective-permute-start(f32[1,16,256]{2,1,0:T(8,128)S(1)} %get-tuple-element.153), channel_id=1, source_target_pairs={{0,8},{8,16},{16,24},{24,32},{32,40},{40,48},{48,56},{56,64},{64,7... | collective-permute-start | bytes 49160 | tf_op jit(solution)/shard_map/ppermute | solution.py:17
  308.4 8.4 %collective-permute-start.33 = (f32[1,16,256]{2,1,0:T(8,128)S(1)}, f32[1,16,256]{2,1,0:T(8,128)S(1)}, u32[]{:S(2)}, u32[]{:S(2)}) collective-permute-start(f32[1,16,256]{2,1,0:T(8,128)S(1)} %get-tuple-element.154), channel_id=1, source_target_pairs={{8,0},{16,8},{24,16},{32,24},{40,32},{48,40},{56,48},{64,56},{72,6... | collective-permute-start | bytes 49160 | tf_op jit(solution)/shard_map/ppermute | solution.py:18
  312.6 68.0 %collective-permute-start.54 = (f32[3,1,128]{2,1,0:T(1,128)S(1)}, f32[3,1,128]{2,1,0:T(1,128)S(1)}, u32[]{:S(2)}, u32[]{:S(2)}) collective-permute-start(f32[3,1,128]{2,1,0:T(1,128)S(1)} %get-tuple-element.173), channel_id=1, source_target_pairs={{0,1},{1,2},{2,3},{3,4},{4,5},{5,6},{6,7},{8,9},{9,10},{10,11},{11... | collective-permute-start | bytes 4616 | tf_op jit(solution)/shard_map/ppermute | solution.py:17
  321.8 58.8 %collective-permute-start.55 = (f32[3,1,128]{2,1,0:T(1,128)S(1)}, f32[3,1,128]{2,1,0:T(1,128)S(1)}, u32[]{:S(2)}, u32[]{:S(2)}) collective-permute-start(f32[3,1,128]{2,1,0:T(1,128)S(1)} %get-tuple-element.174), channel_id=1, source_target_pairs={{1,0},{2,1},{3,2},{4,3},{5,4},{6,5},{7,6},{9,8},{10,9},{11,10},{12... | collective-permute-start | bytes 4616 | tf_op jit(solution)/shard_map/ppermute | solution.py:18
  327.8 6.6 collective-permute-start.37
  345.7 6.6 collective-permute-start.41
  362.4 6.6 collective-permute-start.45
  383.4 6.5 collective-permute-start.57
  400.7 6.5 collective-permute-start.61
  417.9 6.5 collective-permute-start.65
  504.4 6.6 collective-permute-start.85
  521.1 6.6 collective-permute-start.89
  537.8 6.6 collective-permute-start.93
  554.5 6.6 collective-permute-start.97
  572.7 9.1 %collective-permute-start.100 = (f32[1,32,512]{1,2,0:T(8,128)}, f32[1,32,512]{1,2,0:T(8,128)S(1)}, u32[]{:S(2)}, u32[]{:S(2)}) collective-permute-start(f32[1,32,512]{1,2,0:T(8,128)} %get-tuple-element.28), channel_id=1, source_target_pairs={{0,8},{8,16},{16,24},{24,32},{32,40},{40,48},{48,56},{56,64},{64,7... | collective-permute-start | bytes 196616 | tf_op jit(solution)/shard_map/ppermute | solution.py:17
  574.7 11.0 %collective-permute-start.101 = (f32[1,32,512]{1,2,0:T(8,128)}, f32[1,32,512]{1,2,0:T(8,128)}, u32[]{:S(2)}, u32[]{:S(2)}) collective-permute-start(f32[1,32,512]{1,2,0:T(8,128)} %get-tuple-element.29), channel_id=1, source_target_pairs={{8,0},{16,8},{24,16},{32,24},{40,32},{48,40},{56,48},{64,56},{72,6... | collective-permute-start | bytes 196616 | tf_op jit(solution)/shard_map/ppermute | solution.py:18
  586.7 9.0 %collective-permute-start.102 = (f32[6,1,512]{2,1,0:T(1,128)S(1)}, f32[6,1,512]{2,1,0:T(1,128)S(1)}, u32[]{:S(2)}, u32[]{:S(2)}) collective-permute-start(f32[6,1,512]{2,1,0:T(1,128)S(1)} %get-tuple-element.70), channel_id=1, source_target_pairs={{0,1},{1,2},{2,3},{3,4},{4,5},{5,6},{6,7},{8,9},{9,10},{10,11},{11... | collective-permute-start | bytes 36872 | tf_op jit(solution)/shard_map/ppermute | solution.py:17
  607.4 9.1 %collective-permute-start.104 = (f32[1,32,512]{1,2,0:T(8,128)}, f32[1,32,512]{1,2,0:T(8,128)S(1)}, u32[]{:S(2)}, u32[]{:S(2)}) collective-permute-start(f32[1,32,512]{1,2,0:T(8,128)} %get-tuple-element.24), channel_id=1, source_target_pairs={{0,8},{8,16},{16,24},{24,32},{32,40},{40,48},{48,56},{56,64},{64,7... | collective-permute-start | bytes 196616 | tf_op jit(solution)/shard_map/ppermute | solution.py:17
  609.3 10.9 %collective-permute-start.105 = (f32[1,32,512]{1,2,0:T(8,128)}, f32[1,32,512]{1,2,0:T(8,128)}, u32[]{:S(2)}, u32[]{:S(2)}) collective-permute-start(f32[1,32,512]{1,2,0:T(8,128)} %get-tuple-element.25), channel_id=1, source_target_pairs={{8,0},{16,8},{24,16},{32,24},{40,32},{48,40},{56,48},{64,56},{72,6... | collective-permute-start | bytes 196616 | tf_op jit(solution)/shard_map/ppermute | solution.py:18
  621.3 9.0 %collective-permute-start.106 = (f32[6,1,512]{2,1,0:T(1,128)S(1)}, f32[6,1,512]{2,1,0:T(1,128)S(1)}, u32[]{:S(2)}, u32[]{:S(2)}) collective-permute-start(f32[6,1,512]{2,1,0:T(1,128)S(1)} %get-tuple-element.66), channel_id=1, source_target_pairs={{0,1},{1,2},{2,3},{3,4},{4,5},{5,6},{6,7},{8,9},{9,10},{10,11},{11... | collective-permute-start | bytes 36872 | tf_op jit(solution)/shard_map/ppermute | solution.py:17
  642.0 9.1 %collective-permute-start.108 = (f32[1,32,512]{1,2,0:T(8,128)}, f32[1,32,512]{1,2,0:T(8,128)S(1)}, u32[]{:S(2)}, u32[]{:S(2)}) collective-permute-start(f32[1,32,512]{1,2,0:T(8,128)} %get-tuple-element.20), channel_id=1, source_target_pairs={{0,8},{8,16},{16,24},{24,32},{32,40},{40,48},{48,56},{56,64},{64,7... | collective-permute-start | bytes 196616 | tf_op jit(solution)/shard_map/ppermute | solution.py:17
  643.9 10.9 %collective-permute-start.109 = (f32[1,32,512]{1,2,0:T(8,128)}, f32[1,32,512]{1,2,0:T(8,128)}, u32[]{:S(2)}, u32[]{:S(2)}) collective-permute-start(f32[1,32,512]{1,2,0:T(8,128)} %get-tuple-element.21), channel_id=1, source_target_pairs={{8,0},{16,8},{24,16},{32,24},{40,32},{48,40},{56,48},{64,56},{72,6... | collective-permute-start | bytes 196616 | tf_op jit(solution)/shard_map/ppermute | solution.py:18
  655.9 9.0 %collective-permute-start.110 = (f32[6,1,512]{2,1,0:T(1,128)S(1)}, f32[6,1,512]{2,1,0:T(1,128)S(1)}, u32[]{:S(2)}, u32[]{:S(2)}) collective-permute-start(f32[6,1,512]{2,1,0:T(1,128)S(1)} %get-tuple-element.62), channel_id=1, source_target_pairs={{0,1},{1,2},{2,3},{3,4},{4,5},{5,6},{6,7},{8,9},{9,10},{10,11},{11... | collective-permute-start | bytes 36872 | tf_op jit(solution)/shard_map/ppermute | solution.py:17
  676.6 9.1 %collective-permute-start.112 = (f32[1,32,512]{1,2,0:T(8,128)}, f32[1,32,512]{1,2,0:T(8,128)S(1)}, u32[]{:S(2)}, u32[]{:S(2)}) collective-permute-start(f32[1,32,512]{1,2,0:T(8,128)} %get-tuple-element.16), channel_id=1, source_target_pairs={{0,8},{8,16},{16,24},{24,32},{32,40},{40,48},{48,56},{56,64},{64,7... | collective-permute-start | bytes 196616 | tf_op jit(solution)/shard_map/ppermute | solution.py:17
  678.5 10.9 %collective-permute-start.113 = (f32[1,32,512]{1,2,0:T(8,128)}, f32[1,32,512]{1,2,0:T(8,128)}, u32[]{:S(2)}, u32[]{:S(2)}) collective-permute-start(f32[1,32,512]{1,2,0:T(8,128)} %get-tuple-element.17), channel_id=1, source_target_pairs={{8,0},{16,8},{24,16},{32,24},{40,32},{48,40},{56,48},{64,56},{72,6... | collective-permute-start | bytes 196616 | tf_op jit(solution)/shard_map/ppermute | solution.py:18
  690.5 9.0 %collective-permute-start.114 = (f32[6,1,512]{2,1,0:T(1,128)S(1)}, f32[6,1,512]{2,1,0:T(1,128)S(1)}, u32[]{:S(2)}, u32[]{:S(2)}) collective-permute-start(f32[6,1,512]{2,1,0:T(1,128)S(1)} %get-tuple-element.58), channel_id=1, source_target_pairs={{0,1},{1,2},{2,3},{3,4},{4,5},{5,6},{6,7},{8,9},{9,10},{10,11},{11... | collective-permute-start | bytes 36872 | tf_op jit(solution)/shard_map/ppermute | solution.py:17
  711.2 9.1 %collective-permute-start.116 = (f32[1,32,512]{1,2,0:T(8,128)}, f32[1,32,512]{1,2,0:T(8,128)S(1)}, u32[]{:S(2)}, u32[]{:S(2)}) collective-permute-start(f32[1,32,512]{1,2,0:T(8,128)} %get-tuple-element.12), channel_id=1, source_target_pairs={{0,8},{8,16},{16,24},{24,32},{32,40},{40,48},{48,56},{56,64},{64,7... | collective-permute-start | bytes 196616 | tf_op jit(solution)/shard_map/ppermute | solution.py:17
  713.1 10.9 %collective-permute-start.117 = (f32[1,32,512]{1,2,0:T(8,128)}, f32[1,32,512]{1,2,0:T(8,128)}, u32[]{:S(2)}, u32[]{:S(2)}) collective-permute-start(f32[1,32,512]{1,2,0:T(8,128)} %get-tuple-element.13), channel_id=1, source_target_pairs={{8,0},{16,8},{24,16},{32,24},{40,32},{48,40},{56,48},{64,56},{72,6... | collective-permute-start | bytes 196616 | tf_op jit(solution)/shard_map/ppermute | solution.py:18
  725.1 9.0 %collective-permute-start.118 = (f32[6,1,512]{2,1,0:T(1,128)S(1)}, f32[6,1,512]{2,1,0:T(1,128)S(1)}, u32[]{:S(2)}, u32[]{:S(2)}) collective-permute-start(f32[6,1,512]{2,1,0:T(1,128)S(1)} %get-tuple-element.54), channel_id=1, source_target_pairs={{0,1},{1,2},{2,3},{3,4},{4,5},{5,6},{6,7},{8,9},{9,10},{10,11},{11... | collective-permute-start | bytes 36872 | tf_op jit(solution)/shard_map/ppermute | solution.py:17
  (105 other events, 1025.2 us)
where the time goes:
time: 762 us; the launch traced here: 748 us
  starting transfers between devices  335 us (44%)
  local copies, waits for them, and re-layouts  176 us (23%)
  waiting for transfers between devices  138 us (18%)
  other arithmetic  96.1 us (13%)
    ppermute x60, starting transfers between devices, with_halo(): before = lax.ppermute(last, axis, up)  184 us
    ppermute x60, starting transfers between devices, with_halo(): after = lax.ppermute(first, axis, down)  151 us
    ppermute x60, waiting for transfers between devices, with_halo(): after = lax.ppermute(first, axis, down)  118 us
    unnamed x128, local copies, waits for them, and re-layouts  64.7 us
    select_n x24, other arithmetic, colour_pass(): return jnp.where(parity == colour, updated, centre)  50.1 us
    slice x25, local copies, waits for them, and re-layouts, neighbours(): lower_z = jnp.concatenate([zero_plane, centre[:, :, :-1]], axis=2)  29.9 us
    ppermute x60, waiting for transfers between devices, with_halo(): before = lax.ppermute(last, axis, up)  19.7 us
    reshape x1, local copies, waits for them, and re-layouts, restrict_mean(): field.reshape(size_x // 2, 2, size_y // 2, 2, size_z // 2, 2)  18.1 us
  transfers between devices with their start and end apart: 120, of which 48 were waited for; matrix products, arithmetic and copies ran while one was open for 25% of the time, Pallas kernels for 0%

commit v1 on v0

v1 whole, which is shorter than its diff:
```python
import functools

import jax
import jax.numpy as jnp
import numpy as np
from jax import lax
from jax.experimental import pallas as pl
from jax.experimental.pallas import tpu as pltpu
from jax.sharding import PartitionSpec as P

MESH = pl.DeviceIdType.MESH
F32 = jnp.float32
LANES = 128
SUB = 8
PAD2 = 3
MIXED = np.float32(2000.0) / np.float32(1001.0)
NEAR = [(a, b) for a in (-1, 0, 1) for b in (-1, 0, 1) if (a, b) != (0, 0)]


def lanes_of(shape):
    return lax.broadcasted_iota(jnp.int32, shape, len(shape) - 1)


def roll(value, shift, axis):
    size = value.shape[axis]
    return pltpu.roll(value, shift % size, axis)


def split_lanes(tiles):
    shape = tiles[0].shape
    lane = lanes_of(shape)
    block = lane // 32
    within = lane % 32
    parts = [
        jnp.take_along_axis(tiles[t], 4 * within + (block + 4 - t) % 4, axis=1) for t in range(4)
    ]
    out = []
    for k in range(4):
        pick = parts[(3 - k) % 4]
        for b in (2, 1, 0):
            pick = jnp.where(block == b, parts[(b - k) % 4], pick)
        out.append(pick if k == 0 else roll(pick, -32 * k, 1))
    return out


def join_lanes(quarters):
    shape = quarters[0].shape
    lane = lanes_of(shape)
    block = lane // 32
    turned = [quarters[k] if k == 0 else roll(quarters[k], 32 * k, 1) for k in range(4)]
    out = []
    for t in range(4):
        pick = turned[(3 - t) % 4]
        for b in (2, 1, 0):
            pick = jnp.where(block == b, turned[(b - t) % 4], pick)
        out.append(jnp.take_along_axis(pick, ((lane % 4 + t) % 4) * 32 + lane // 4, axis=1))
    return out


def planes(low, high, body):
    count = high - low
    if count % 2 == 0 and count > 2:

        def pair(i, carry):
            body(low + 2 * i, low % 2)
            body(low + 2 * i + 1, (low + 1) % 2)
            return carry

        lax.fori_loop(0, count // 2, pair, 0)
    else:
        for x in range(low, high):
            body(x, x % 2)


class Level:
    def __init__(self, rows, pairs, refs, face):
        self.rows, self.pairs, self.face = rows, pairs, face
        self.v, self.s, self.m, self.cx, self.cy, self.cz, self.cyl, self.czl, self.d, self.inv = refs

    def bit(self, c, par, r):
        return (c + par + 1 + r) % 2

    def load(self, ref, x, c, par, r, start, stride):
        b = self.bit(c, par, r)
        return [ref[x, 2 * j + b, pl.ds(start, SUB, stride=stride), :] for j in range(self.pairs)]

    def z_shift_up(self, values, b):
        if b == 0:
            return values
        return values[1:] + [roll(values[0], -1, 1)]

    def z_shift_down(self, values, b):
        if b == 1:
            return values
        return [roll(values[-1], 1, 1)] + values[:-1]

    def get(self, ref, c, x, r):
        return [ref[c, x, r, j] for j in range(self.pairs)]

    def y_up(self, ref, c, x, r):
        if r < self.rows - 1:
            return self.get(ref, c, x, r + 1)
        return [roll(v, -1, 0) for v in self.get(ref, c, x, 0)]

    def y_down(self, ref, c, x, r):
        if r > 0:
            return self.get(ref, c, x, r - 1)
        return [roll(v, 1, 0) for v in self.get(ref, c, x, self.rows - 1)]

    def faces_x(self, low, high):
        def body(x, par):
            for c in (0, 1):
                for r in range(self.rows):
                    here, there = self.get(self.m, c, x, r), self.get(self.m, 1 - c, x + 1, r)
                    for j in range(self.pairs):
                        self.cx[c, x, r, j] = self.face(here[j], there[j])

        planes(low, high, body)

    def faces_yz(self, low, high):
        last = lanes_of((SUB, LANES)) == LANES - 1

        def body(x, par):
            for c in (0, 1):
                for r in range(self.rows):
                    b = self.bit(c, par, r)
                    here = self.get(self.m, c, x, r)
                    there = self.y_up(self.m, 1 - c, x, r)
                    above = self.z_shift_up(self.get(self.m, 1 - c, x, r), b)
                    for j in range(self.pairs):
                        self.cy[c, x, r, j] = self.face(here[j], there[j])
                        up = self.face(here[j], above[j])
                        if b == 1 and j == self.pairs - 1:
                            up = jnp.where(last, 0.0, up)
                        self.cz[c, x, r, j] = up

        planes(low, high, body)

    def diagonals(self, low, high):
        last = lanes_of((SUB, LANES)) == LANES - 1

        def body(x, par):
            for c in (0, 1):
                for r in range(self.rows):
                    b = self.bit(c, par, r)
                    xl, xu = self.get(self.cx, 1 - c, x - 1, r), self.get(self.cx, c, x, r)
                    yl, yu = self.y_down(self.cy, 1 - c, x, r), self.get(self.cy, c, x, r)
                    zl = self.z_shift_down(self.get(self.cz, 1 - c, x, r), b)
                    zu = self.get(self.cz, c, x, r)
                    for j in range(self.pairs):
                        if r == 0:
                            self.cyl[c, x, j] = yl[j]
                        if b == 0 and j == 0:
                            self.czl[c, x, r] = zl[j]
                        total = xl[j] + xu[j] + yl[j] + yu[j] + zl[j] + zu[j]
                        if b == 1 and j == self.pairs - 1:
                            total = total + jnp.where(last, 2.0 * self.m[c, x, r, j], 0.0)
                        total = jnp.where(total > 0, total, 1.0)
                        self.d[c, x, r, j] = total
                        self.inv[c, x, r, j] = 1.0 / total

        planes(low, high, body)

    def beside(self, c, x, par, r):
        o = 1 - c
        b = self.bit(c, par, r)
        same = self.get(self.v, o, x, r)
        parts = [
            (self.get(self.cx, o, x - 1, r), self.get(self.v, o, x - 1, r)),
            (self.get(self.cx, c, x, r), self.get(self.v, o, x + 1, r)),
            (
                self.get(self.cy, o, x, r - 1) if r else [self.cyl[c, x, j] for j in range(self.pairs)],
                self.y_down(self.v, o, x, r),
            ),
            (self.get(self.cy, c, x, r), self.y_up(self.v, o, x, r)),
        ]
        lower = self.get(self.cz, o, x, r)
        if b == 0:
            lower = [self.czl[c, x, r]] + lower[:-1]
        parts.append((lower, self.z_shift_down(same, b)))
        parts.append((self.get(self.cz, c, x, r), self.z_shift_up(same, b)))
        out = []
        for j in range(self.pairs):
            terms = [k[j] * v[j] for k, v in parts]
            out.append((terms[0] + terms[1]) + (terms[2] + terms[3]) + (terms[4] + terms[5]))
        return out

    def colour_pass(self, c, low, high):
        def body(x, par):
            for r in range(self.rows):
                total = self.beside(c, x, par, r)
                for j in range(self.pairs):
                    self.v[c, x, r, j] = (self.s[c, x, r, j] + total[j]) * self.inv[c, x, r, j]

        planes(low, high, body)

    def residual(self, c, x, par, r):
        total = self.beside(c, x, par, r)
        return [
            self.s[c, x, r, j] - (self.d[c, x, r, j] * self.v[c, x, r, j] - total[j])
            for j in range(self.pairs)
        ]


def face_fine(left, right):
    both = left * right
    return jnp.where(both > 1e5, 1000.0, jnp.where(both > 500.0, MIXED, both))


def face_coarse(left, right):
    return 2.0 * left * right / jnp.maximum(left + right, 0.5)


class Wire:
    def __init__(self, ng, ny, send, recv):
        self.ng, self.ny, self.send, self.recv, self.used = ng, ny, send, recv, 0
        self.g, self.y = lax.axis_index("gx"), lax.axis_index("yz")

    def inside(self, dg, dy):
        g, y = self.g + dg, self.y + dy
        return (g >= 0) & (g < self.ng) & (y >= 0) & (y < self.ny)

    def copy(self, src, dst, dg, dy):
        k = self.used
        self.used += 1
        made = pltpu.make_async_remote_copy(
            src_ref=src,
            dst_ref=dst,
            send_sem=self.send.at[k],
            recv_sem=self.recv.at[k],
            device_id=(self.g + dg, self.y + dy),
            device_id_type=MESH,
        )
        return (made, dst, dg, dy)

    def start(self, copies):
        for made, _, dg, dy in copies:
            pl.when(self.inside(dg, dy))(made.start)

    def arrive(self, copies, fill=0):
        for made, dst, dg, dy in copies:
            there = self.inside(-dg, -dy)
            pl.when(there)(made.wait_recv)
            if fill is not None:

                @pl.when(jnp.logical_not(there))
                def _(dst=dst):
                    dst[...] = jnp.full(dst.shape, fill, dst.dtype)

    def sent(self, copies):
        for made, _, dg, dy in copies:
            pl.when(self.inside(dg, dy))(made.wait_send)


def fine_blocks(wire, src, dst, low, high, directions):
    out = []
    for dg, dy in directions:
        if dg == 1:
            xs, xd = pl.ds(4 - high, high - low), pl.ds(3 - high, high - low)
        elif dg == -1:
            xs, xd = pl.ds(low, high - low), pl.ds(7 + low, high - low)
        else:
            xs, xd = pl.ds(0, 4), pl.ds(3, 4)
        ys, yd = ((0, 8), (40, 8)) if dy == -1 else ((24, 8), (0, 8)) if dy == 1 else ((0, 32), (8, 32))
        out.append(wire.copy(src.at[xs, pl.ds(*ys), :], dst.at[xd, pl.ds(*yd), :], dg, dy))
    return out


def middle_blocks(wire, src, dst, reach):
    out = []
    for dg in range(-3, 4):
        for dy in (-1, 0, 1):
            if (dg, dy) == (0, 0) or 2 * abs(dg) - 1 > reach:
                continue
            if abs(dg) == 3:
                xs, xd = (pl.ds(1, 1), pl.ds(0, 1)) if dg == 3 else (pl.ds(0, 1), pl.ds(11, 1))
            else:
                xs, xd = pl.ds(0, 2), pl.ds(5 - 2 * dg, 2)
            ys, yd = ((8, 8), (24, 8)) if dy == -1 else ((16, 8), (0, 8)) if dy == 1 else ((8, 16), (8, 16))
            out.append(
                wire.copy(src.at[xs, :, pl.ds(*ys), :], dst.at[xd, :, pl.ds(*yd), :], dg, dy)
            )
    return out


class Gather:
    def __init__(self, wire, src, dst):
        self.wire, self.src, self.dst = wire, src, dst
        self.first = wire.used
        self.n = wire.ng
        wire.used += self.n - 1
        self.rows = pl.ds(16, 8)
        self.along = []

    def hop(self, d, plane):
        wire = self.wire
        return pltpu.make_async_remote_copy(
            src_ref=self.src,
            dst_ref=self.dst.at[PAD2 + plane, self.rows, :],
            send_sem=wire.send.at[self.first + d - 1],
            recv_sem=wire.recv.at[self.first + d - 1],
            device_id=((wire.g + d) % self.n, wire.y),
            device_id_type=MESH,
        )

    def start(self):
        for d in range(1, self.n):
            self.hop(d, self.wire.g).start()

    def forward(self):
        for d in range(1, self.n):
            self.hop(d, (self.wire.g + self.n - d) % self.n).wait_recv()
        for dy in (-1, 1, -2, 2):
            span = pl.ds(PAD2, self.n)
            self.along.append(
                self.wire.copy(
                    self.dst.at[span, self.rows, :],
                    self.dst.at[span, pl.ds(16 - 8 * dy, 8), :],
                    0,
                    dy,
                )
            )
        self.wire.start(self.along)

    def finish(self):
        self.wire.arrive(self.along)

    def sent(self):
        for d in range(1, self.n):
            self.hop(d, self.wire.g).wait_send()
        self.wire.sent(self.along)


def kernel(
    ng, ny,
    rhs, phase, guess, p_out, r_out,
    in_phase, in_guess, in_rhs, rows_a, rows_b, rows_c,
    v0, s0, m0, cx0, cy0, cz0, cyl0, czl0, d0, inv0,
    v1, s1, m1, cx1, cy1, cz1, cyl1, czl1, d1, inv1,
    v2, s2, m2, cx2, cy2, cz2, cyl2, czl2, inv2,
    send_m1, send_s1, send_e1, wide_m1, wide_s1, wide_e1,
    send_m2, send_s2, wide_m2, wide_s2, rows_e2, rows_eb,
    got_low, got_high, last_low, last_high, far_low, far_high,
    rows_p, rows_far, p_vm, r_vm,
    local, out_sem, send, recv,
):
    wire = Wire(ng, ny, send, recv)
    g, y = wire.g, wire.y
    fine = Level(6, 2, (v0, s0, m0, cx0, cy0, cz0, cyl0, czl0, d0, inv0), face_fine)
    mid = Level(4, 1, (v1, s1, m1, cx1, cy1, cz1, cyl1, czl1, d1, inv1), face_coarse)

    own = (pl.ds(3, 4), pl.ds(8, 32))
    loads = [
        pltpu.make_async_copy(src, dst.at[own[0], own[1], :], local.at[i])
        for i, (src, dst) in enumerate(((phase, in_phase), (guess, in_guess), (rhs, in_rhs)))
    ]
    for load in loads:
        load.start()

    barrier = pltpu.get_barrier_semaphore()
    peers = [(dg, dy) for dg in range(-3, 4) for dy in (-1, 0, 1) if dy != 0 or dg == 0]
    peers = [p for p in peers if p != (0, 0)] + [(0, -2), (0, 2)]
    count = jnp.int32(ng - 1)
    for dg, dy in peers:
        there = wire.inside(dg, dy)
        count = count + there.astype(jnp.int32)

        @pl.when(there)
        def _(dg=dg, dy=dy):
            pl.semaphore_signal(barrier, inc=1, device_id=(g + dg, y + dy), device_id_type=MESH)

    for d in range(1, ng):
        pl.semaphore_signal(barrier, inc=1, device_id=((g + d) % ng, y), device_id_type=MESH)
    pl.semaphore_wait(barrier, count)

    side = [d for d in NEAR if d[0] != 0]
    phase_first = fine_blocks(wire, phase, in_phase, 0, 2, NEAR)
    guess_first = fine_blocks(wire, guess, in_guess, 0, 2, NEAR)
    rhs_first = fine_blocks(wire, rhs, in_rhs, 0, 1, NEAR)
    phase_more = fine_blocks(wire, phase, in_phase, 2, 3, side)
    rhs_more = fine_blocks(wire, rhs, in_rhs, 1, 2, side)
    for group in (phase_first, guess_first, rhs_first, phase_more, rhs_more):
        wire.start(group)

    def unpack(src, dst, low, high, first, count):
        rows = pl.ds(first, count)

        def body(x, carry):
            tiles = [src[x, rows, pl.ds(LANES * t, LANES)] for t in range(4)]
            for q, part in enumerate(split_lanes(tiles)):
                dst[x, q, rows, :] = part
            return carry

        lax.fori_loop(low, high, body, 0)

    def unpack_phase(low, high, first, count):
        rows = pl.ds(first, count)

        def body(x, carry):
            tiles = []
            for t in range(4):
                tile = in_phase[x, rows, pl.ds(LANES * t, LANES)]
                value = jnp.where(tile > 0, 1000.0, 1.0)
                tiles.append(jnp.where(tile < 0, 0.0, value))
            for q, part in enumerate(split_lanes(tiles)):
                rows_a[x, q, rows, :] = part
            return carry

        lax.fori_loop(low, high, body, 0)

    def dense(ref, rows, low, high, colours):
        def body(x, par):
            for c in colours:
                for r in range(6):
                    values = fine.load(rows, x, c, par, r, r, 6)
                    for j in range(2):
                        ref[c, x, r, j] = values[j]

        planes(low, high, body)

    loads[0].wait()
    unpack_phase(3, 7, 8, 32)
    coarsest = None
    for big in range(2):
        for q in range(2):
            for half in range(2):
                total = None
                for x in (3 + 2 * big, 4 + 2 * big):
                    for k in (0, 1):
                        for r in (2 * half, 2 * half + 1):
                            part = rows_a[x, 2 * q + k, pl.ds(8 + r, SUB, stride=4), :]
                            total = part if total is None else total + part
                total = 0.125 * total
                send_m1[big, q, pl.ds(8 + half, SUB, stride=2), :] = total
                coarsest = total if coarsest is None else coarsest + total
    coarsest = 0.125 * coarsest
    send_m2[...] = coarsest
    wide_m2[PAD2 + g, pl.ds(16, 8), :] = coarsest
    wide_m1[pl.ds(5, 2), :, pl.ds(8, 16), :] = send_m1[:, :, pl.ds(8, 16), :]

    loads[1].wait()
    unpack(in_guess, rows_b, 3, 7, 8, 32)
    loads[2].wait()
    unpack(in_rhs, rows_c, 3, 7, 8, 32)

    wire.arrive(phase_first, -1)
    for x in range(1, 9):
        if 3 <= x < 7:
            continue
        unpack_phase(x, x + 1, 0, 48)
    unpack_phase(3, 7, 0, 8)
    unpack_phase(3, 7, 40, 8)
    dense(m0, rows_a, 1, 9, (0, 1))
    fine.faces_x(1, 8)
    fine.faces_yz(2, 8)
    fine.diagonals(2, 8)

    wire.arrive(guess_first)
    unpack(in_guess, rows_b, 1, 3, 0, 48)
    unpack(in_guess, rows_b, 7, 9, 0, 48)
    unpack(in_guess, rows_b, 3, 7, 0, 8)
    unpack(in_guess, rows_b, 3, 7, 40, 8)
    dense(v0, rows_b, 1, 9, (1,))
    wire.arrive(rhs_first)
    unpack(in_rhs, rows_c, 2, 3, 0, 48)
    unpack(in_rhs, rows_c, 7, 8, 0, 48)
    unpack(in_rhs, rows_c, 3, 7, 0, 8)
    unpack(in_rhs, rows_c, 3, 7, 40, 8)
    dense(s0, rows_c, 2, 8, (0, 1))

    def sweep_one():
        fine.colour_pass(0, 2, 8)
        fine.colour_pass(1, 3, 7)

    def exchange(low, high):
        copies = [
            wire.copy(v0.at[1, pl.ds(4, 3)], low, 1, 0),
            wire.copy(v0.at[1, pl.ds(3, 3)], high, -1, 0),
        ]
        wire.start(copies)
        return copies

    def sweep_two(copies, low, high):
        wire.arrive(copies)
        v0[1, pl.ds(0, 3)] = low[...]
        v0[1, pl.ds(7, 3)] = high[...]
        fine.colour_pass(0, 1, 9)
        wire.sent(copies)
        fine.colour_pass(1, 2, 8)

    sweep_one()
    swap = exchange(got_low, got_high)
    m1_blocks = middle_blocks(wire, send_m1, wide_m1, 5)
    wire.start(m1_blocks)
    m2_all = Gather(wire, send_m2, wide_m2)
    m2_all.start()

    wire.arrive(phase_more, -1)
    unpack_phase(0, 1, 0, 48)
    unpack_phase(9, 10, 0, 48)
    dense(m0, rows_a, 0, 1, (0, 1))
    dense(m0, rows_a, 9, 10, (0, 1))
    fine.faces_x(0, 1)
    fine.faces_x(8, 9)
    fine.faces_yz(1, 2)
    fine.faces_yz(8, 9)
    fine.diagonals(1, 2)
    fine.diagonals(8, 9)
    wire.arrive(rhs_more)
    unpack(in_rhs, rows_c, 1, 2, 0, 48)
    unpack(in_rhs, rows_c, 8, 9, 0, 48)
    dense(s0, rows_c, 1, 2, (0, 1))
    dense(s0, rows_c, 8, 9, (0, 1))

    sweep_two(swap, got_low, got_high)

    for big in range(2):
        for r1 in range(3):
            total = [None, None]
            for x in (3 + 2 * big, 4 + 2 * big):
                for r in (2 * r1, 2 * r1 + 1):
                    for c in (0, 1):
                        part = fine.residual(c, x, x % 2, r)
                        for j in range(2):
                            total[j] = part[j] if total[j] is None else total[j] + part[j]
            for j in range(2):
                send_s1[big, j, pl.ds(4 + r1, SUB, stride=3), :] = 0.5 * total[j]
    s1_blocks = middle_blocks(wire, send_s1, wide_s1, 4)
    wire.start(s1_blocks)
    wide_s1[pl.ds(5, 2), :, pl.ds(8, 16), :] = send_s1[:, :, pl.ds(8, 16), :]

    for x in range(3, 7):
        for c in (0, 1):
            for r in range(6):
                b = fine.bit(c, x % 2, r)
                for j in range(2):
                    rows_p[x - 3, 2 * j + b, pl.ds(r, SUB, stride=6), :] = v0[c, x, r, j]
    far = [
        wire.copy(v0.at[1, pl.ds(5, 1)], far_low, 1, 0),
        wire.copy(v0.at[1, pl.ds(4, 1)], far_high, -1, 0),
        wire.copy(rows_p.at[:, :, pl.ds(32, 8), :], rows_far.at[:, :, pl.ds(0, 8), :], 0, 1),
        wire.copy(rows_p.at[:, :, pl.ds(8, 8), :], rows_far.at[:, :, pl.ds(40, 8), :], 0, -1),
    ]
    wire.start(far)

    wire.arrive(m1_blocks)

    def dense_mid(ref, rows, low, high, colours):
        def body(x, par):
            for c in colours:
                for r in range(4):
                    ref[c, x, r, 0] = mid.load(rows, x, c, par, r, r, 4)[0]

        planes(low, high, body)

    dense_mid(m1, wide_m1, 0, 12, (0, 1))
    mid.faces_x(0, 11)
    mid.faces_yz(1, 11)
    mid.diagonals(1, 11)
    m2_all.forward()
    v1[1] = jnp.zeros(v1.shape[1:], F32)

    def sweeps_mid():
        mid.colour_pass(0, 1, 11)
        mid.colour_pass(1, 2, 10)
        mid.colour_pass(0, 3, 9)
        mid.colour_pass(1, 4, 8)

    wire.arrive(s1_blocks)
    dense_mid(s1, wide_s1, 1, 11, (0, 1))
    sweeps_mid()
    for r2 in range(2):
        total = None
        for x in (5, 6):
            for r in (2 * r2, 2 * r2 + 1):
                for c in (0, 1):
                    part = mid.residual(c, x, x % 2, r)[0]
                    total = part if total is None else total + part
        send_s2[pl.ds(4 + r2, SUB, stride=2), :] = 0.5 * total
    s2_all = Gather(wire, send_s2.at[pl.ds(8, 8), :], wide_s2)
    s2_all.start()
    wide_s2[PAD2 + g, pl.ds(16, 8), :] = send_s2[pl.ds(8, 8), :]
    for x in (5, 6):
        for c in (0, 1):
            for r in range(4):
                b = mid.bit(c, x % 2, r)
                send_e1[x - 5, b, pl.ds(r, SUB, stride=4), :] = v1[c, x, r, 0]
    e1_blocks = middle_blocks(wire, send_e1, wide_e1, 5)
    wire.start(e1_blocks)
    wide_e1[pl.ds(5, 2), :, pl.ds(8, 16), :] = send_e1[:, :, pl.ds(8, 16), :]

    m2_all.finish()
    lane = lanes_of((SUB, LANES))
    last = lane == LANES - 1
    zero = jnp.zeros((SUB, LANES), F32)
    for x in range(PAD2):
        for r in range(4):
            for ref in (v2, m2, cx2):
                ref[x, r] = zero
                ref[PAD2 + ng + x, r] = zero

    def load_two(ref, rows):
        def body(x, carry):
            for r in range(4):
                ref[x, r] = rows[x, pl.ds(4 + r, SUB, stride=4), :]
            return carry

        lax.fori_loop(PAD2, PAD2 + ng, body, 0)

    load_two(m2, wide_m2)

    def faces_two(x, carry):
        for r in range(4):
            here = m2[x, r]
            cx2[x, r] = face_coarse(here, m2[x + 1, r])
            cy2[x, r] = face_coarse(here, m2[x, r + 1] if r < 3 else roll(m2[x, 0], -1, 0))
            up = jnp.where(last, 0.0, face_coarse(here, roll(here, -1, 1)))
            cz2[x, r] = up
            czl2[x, r] = roll(up, 1, 1)
        cyl2[x] = roll(cy2[x, 3], 1, 0)
        for r in range(4):
            yl = cy2[x, r - 1] if r else cyl2[x]
            total = cx2[x - 1, r] + cx2[x, r] + yl + cy2[x, r] + cz2[x, r] + czl2[x, r]
            total = total + jnp.where(last, 2.0 * m2[x, r], 0.0)
            inv2[x, r] = 1.0 / jnp.where(total > 0, total, 1.0)
            v2[x, r] = zero
        return carry

    lax.fori_loop(PAD2, PAD2 + ng, faces_two, 0)

    s2_all.forward()
    s2_all.finish()
    load_two(s2, wide_s2)

    def pass_two(c):
        def one(x, par):
            field = [v2[x, r] for r in range(4)]
            below, above = roll(field[3], 1, 0), roll(field[0], -1, 0)
            for r in range(4):
                yl = field[r - 1] if r else below
                yu = field[r + 1] if r < 3 else above
                total = cx2[x - 1, r] * v2[x - 1, r] + cx2[x, r] * v2[x + 1, r]
                total = total + ((cy2[x, r - 1] if r else cyl2[x]) * yl + cy2[x, r] * yu)
                total = total + (czl2[x, r] * roll(field[r], 1, 1) + cz2[x, r] * roll(field[r], -1, 1))
                value = (s2[x, r] + total) * inv2[x, r]
                hit = (lane + (par + r + c)) % 2 == 0
                v2[x, r] = jnp.where(hit, value, field[r])

        def pair(i, carry):
            one(PAD2 + 2 * i, 0)
            one(PAD2 + 2 * i + 1, 1)
            return carry

        lax.fori_loop(0, ng // 2, pair, 0)

    def sweep_of_two(i, carry):
        pass_two(0)
        pass_two(1)
        return carry

    lax.fori_loop(0, 4, sweep_of_two, 0)

    def keep_two(x, carry):
        for r in range(4):
            rows_e2[x, pl.ds(r, SUB, stride=4), :] = v2[x, r]
        return carry

    lax.fori_loop(0, ng + 2 * PAD2, keep_two, 0)

    wire.arrive(e1_blocks)
    for x in range(12):
        source = g + ((x + 1) // 2 - 3 + PAD2)
        for r in range(4):
            value = mid.load(wide_e1, x, 1, x % 2, r, r, 4)[0]
            v1[1, x, r, 0] = value + rows_e2[source, pl.ds(8 + r // 2, SUB, stride=2), :]
    sweeps_mid()
    for x in range(4, 8):
        for c in (0, 1):
            for r in range(4):
                b = mid.bit(c, x % 2, r)
                rows_eb[x - 4, b, pl.ds(r, SUB, stride=4), :] = v1[c, x, r, 0]

    wire.arrive(far[2:])
    wire.arrive(far[:2])
    wire.sent(far)
    rows_far[:, :, pl.ds(8, 32), :] = rows_p[:, :, pl.ds(8, 32), :]
    for x in range(3, 7):
        for r in range(6):
            values = fine.load(rows_far, x - 3, 1, x % 2, r, r, 6)
            for j in range(2):
                v0[1, x, r, j] = values[j]
    v0[1, pl.ds(1, 1)] = far_low[...]
    v0[1, pl.ds(8, 1)] = far_high[...]
    for x in range(1, 9):
        for r in range(6):
            for j in range(2):
                add = rows_eb[(x - 1) // 2, j, pl.ds(4 + r // 2, SUB, stride=3), :]
                v0[1, x, r, j] = v0[1, x, r, j] + add
    sweep_one()
    swap_last = exchange(last_low, last_high)
    sweep_two(swap_last, last_low, last_high)

    for x in range(3, 7):
        for c in (0, 1):
            for r in range(6):
                b = fine.bit(c, x % 2, r)
                part = fine.residual(c, x, x % 2, r)
                for j in range(2):
                    rows_p[x - 3, 2 * j + b, pl.ds(r, SUB, stride=6), :] = v0[c, x, r, j]
                    rows_a[x, 2 * j + b, pl.ds(r, SUB, stride=6), :] = part[j]
    for x in range(4):
        for t, tile in enumerate(join_lanes([rows_p[x, q, pl.ds(8, 32), :] for q in range(4)])):
            p_vm[x, :, pl.ds(LANES * t, LANES)] = tile
        for t, tile in enumerate(join_lanes([rows_a[x + 3, q, pl.ds(8, 32), :] for q in range(4)])):
            r_vm[x, :, pl.ds(LANES * t, LANES)] = tile
    outs = [
        pltpu.make_async_copy(p_vm, p_out, out_sem.at[0]),
        pltpu.make_async_copy(r_vm, r_out, out_sem.at[1]),
    ]
    for out in outs:
        out.start()
    for group in (phase_first, guess_first, rhs_first, phase_more, rhs_more, m1_blocks, s1_blocks, e1_blocks):
        wire.sent(group)
    m2_all.sent()
    s2_all.sent()
    for out in outs:
        out.wait()


def scratch(ng):
    vec = lambda *shape: pltpu.VMEM(shape + (SUB, LANES), F32)
    rows = lambda *shape: pltpu.VMEM(shape + (LANES,), F32)
    two = ng + 2 * PAD2
    shapes = [pltpu.VMEM((10, 48, 512), jnp.int32), pltpu.VMEM((10, 48, 512), F32), pltpu.VMEM((10, 48, 512), F32)]
    shapes += [rows(10, 4, 48)] * 3
    for n, r, j in ((10, 6, 2), (12, 4, 1)):
        shapes += [vec(2, n, r, j)] * 6 + [vec(2, n, j), vec(2, n, r)] + [vec(2, n, r, j)] * 2
    shapes += [vec(two, 4)] * 6 + [vec(two)] + [vec(two, 4)] * 2
    shapes += [rows(2, 2, 32)] * 3 + [rows(12, 2, 32)] * 3
    shapes += [rows(8), rows(24), rows(two, 40), rows(two, 40), rows(two, 32), rows(4, 2, 32)]
    shapes += [vec(3, 6, 2)] * 4 + [vec(1, 6, 2)] * 2
    shapes += [rows(4, 4, 48)] * 2 + [pltpu.VMEM((4, 32, 512), F32), pltpu.VMEM((4, 32, 512), F32)]
    count = 160
    shapes += [pltpu.SemaphoreType.DMA((3,)), pltpu.SemaphoreType.DMA((2,))]
    shapes += [pltpu.SemaphoreType.DMA((count,)), pltpu.SemaphoreType.DMA((count,))]
    return shapes


def solution(mesh):
    ng, ny = mesh.shape["gx"], mesh.shape["yz"]

    def local(right_side, phase, pressure_guess):
        anywhere = pl.BlockSpec(memory_space=pl.ANY)
        out = jax.ShapeDtypeStruct(right_side.shape, F32)
        return pl.pallas_call(
            functools.partial(kernel, ng, ny),
            out_shape=(out, out),
            in_specs=[anywhere] * 3,
            out_specs=(anywhere, anywhere),
            scratch_shapes=scratch(ng),
            compiler_params=pltpu.CompilerParams(
                collective_id=0, has_side_effects=True, vmem_limit_bytes=56 * 1024 * 1024
            ),
            name="vcycle",
        )(right_side, phase, pressure_guess)

    specs = P("gx", "yz", None)
    return jax.shard_map(
        local, mesh=mesh, in_specs=(specs,) * 3, out_specs=(specs, specs), check_vma=False
    )
```

time: 762 us -> 72.4 us (0.10)
  the two profiles are of different devices: /device:TPU:97 before, /device:TPU:8 now
where the time goes in v1:
time: 72.4 us; the launch traced here: 72.3 us
  Pallas kernels  69.2 us (96%)
  local copies, waits for them, and re-layouts  2.42 us (3%)
    pallas_call x1, Pallas kernels, local(): pl.pallas_call(functools.partial(kernel, ng, ny), out_shape=(out, out), i...  69.2 us
    unnamed x4, local copies, waits for them, and re-layouts  2.42 us

profile of v1, /device:TPU:8, one launch (start us, length us, event | category | flops | bytes accessed | tf_op | source)
XLA Modules:
  0.0 72.3 jit_solution(10813815699152173621)
XLA Ops:
  0.6 69.2 %vcycle.1 = (f32[4,32,512]{2,1,0:T(8,128)}, f32[4,32,512]{2,1,0:T(8,128)}) custom-call(f32[4,32,512]{2,1,0:T(8,128)} %rhs.1, s32[4,32,512]{2,1,0:T(8,128)} %phase.1, f32[4,32,512]{2,1,0:T(8,128)} %guess.1), custom_call_target="tpu_custom_call" | custom-call | tf_op jit(solution)/shard_map/vcycle/pallas_call | solution.py:755
  69.8 0.0 copy-start
  69.9 1.7 %copy.7 = f32[4,32,512]{2,1,0:T(8,128)} copy(f32[4,32,512]{2,1,0:T(8,128)} %get-tuple-element.4) | data formatting | bytes 524288
  71.6 0.0 copy-done
  71.6 0.7 copy.8
Async XLA Ops:
  69.8 1.7 %copy-start = (f32[4,32,512]{2,1,0:T(8,128)S(1)}, f32[4,32,512]{2,1,0:T(8,128)}, u32[]{:S(2)}) copy-start(f32[4,32,512]{2,1,0:T(8,128)} %get-tuple-element.5) | copy-start | bytes 786436

commit v2 on v1

--- a/solution.py
+++ b/solution.py
@@ -14,7 +14,6 @@
 SUB = 8
 PAD2 = 3
 MIXED = np.float32(2000.0) / np.float32(1001.0)
-NEAR = [(a, b) for a in (-1, 0, 1) for b in (-1, 0, 1) if (a, b) != (0, 0)]
 
 
 def lanes_of(shape):
@@ -73,8 +72,9 @@
 
 
 class Level:
-    def __init__(self, rows, pairs, refs, face):
+    def __init__(self, rows, pairs, refs, face, span=LANES):
         self.rows, self.pairs, self.face = rows, pairs, face
+        self.span = span
         self.v, self.s, self.m, self.cx, self.cy, self.cz, self.cyl, self.czl, self.d, self.inv = refs
 
     def bit(self, c, par, r):
@@ -118,7 +118,7 @@
         planes(low, high, body)
 
     def faces_yz(self, low, high):
-        last = lanes_of((SUB, LANES)) == LANES - 1
+        last = lanes_of((SUB, LANES)) % self.span == self.span - 1
 
         def body(x, par):
             for c in (0, 1):
@@ -137,7 +137,7 @@
         planes(low, high, body)
 
     def diagonals(self, low, high):
-        last = lanes_of((SUB, LANES)) == LANES - 1
+        last = lanes_of((SUB, LANES)) % self.span == self.span - 1
 
         def body(x, par):
             for c in (0, 1):
@@ -215,6 +215,7 @@
     def __init__(self, ng, ny, send, recv):
         self.ng, self.ny, self.send, self.recv, self.used = ng, ny, send, recv, 0
         self.g, self.y = lax.axis_index("gx"), lax.axis_index("yz")
+        self.coming, self.going, self.gathers = [], [], []
 
     def inside(self, dg, dy):
         g, y = self.g + dg, self.y + dy
@@ -236,11 +237,14 @@
     def start(self, copies):
         for made, _, dg, dy in copies:
             pl.when(self.inside(dg, dy))(made.start)
+        self.coming += copies
+        self.going += copies
 
     def arrive(self, copies, fill=0):
         for made, dst, dg, dy in copies:
             there = self.inside(-dg, -dy)
             pl.when(there)(made.wait_recv)
+            self.coming = [c for c in self.coming if c[0] is not made]
             if fill is not None:
 
                 @pl.when(jnp.logical_not(there))
@@ -250,26 +254,45 @@
     def sent(self, copies):
         for made, _, dg, dy in copies:
             pl.when(self.inside(dg, dy))(made.wait_send)
-
-
-def fine_blocks(wire, src, dst, low, high, directions):
+            self.going = [c for c in self.going if c[0] is not made]
+
+    def drain(self):
+        self.arrive(list(self.coming), None)
+        self.sent(list(self.going))
+        for gather in self.gathers:
+            gather.sent()
+
+
+def fine_planes(wire, src, dst, low, high):
+    n = high - low
+    rows = pl.ds(8, 32)
+    return [
+        wire.copy(src.at[pl.ds(4 - high, n)], dst.at[pl.ds(3 - high, n), rows, :], 1, 0),
+        wire.copy(src.at[pl.ds(low, n)], dst.at[pl.ds(7 + low, n), rows, :], -1, 0),
+    ]
+
+
+def fine_rims(wire, src, dst):
+    own = pl.ds(3, 4)
+    return [
+        wire.copy(src.at[:, pl.ds(24, 8), :], dst.at[own, pl.ds(0, 8), :], 0, 1),
+        wire.copy(src.at[:, pl.ds(0, 8), :], dst.at[own, pl.ds(40, 8), :], 0, -1),
+    ]
+
+
+def fine_corners(wire, ref, spans):
     out = []
-    for dg, dy in directions:
-        if dg == 1:
-            xs, xd = pl.ds(4 - high, high - low), pl.ds(3 - high, high - low)
-        elif dg == -1:
-            xs, xd = pl.ds(low, high - low), pl.ds(7 + low, high - low)
-        else:
-            xs, xd = pl.ds(0, 4), pl.ds(3, 4)
-        ys, yd = ((0, 8), (40, 8)) if dy == -1 else ((24, 8), (0, 8)) if dy == 1 else ((0, 32), (8, 32))
-        out.append(wire.copy(src.at[xs, pl.ds(*ys), :], dst.at[xd, pl.ds(*yd), :], dg, dy))
+    for first, n in spans:
+        xs = pl.ds(first, n)
+        out.append(wire.copy(ref.at[xs, pl.ds(32, 8), :], ref.at[xs, pl.ds(0, 8), :], 0, 1))
+        out.append(wire.copy(ref.at[xs, pl.ds(8, 8), :], ref.at[xs, pl.ds(40, 8), :], 0, -1))
     return out
 
 
-def middle_blocks(wire, src, dst, reach):
+def middle_blocks(wire, src, dst, reach, sides=(-1, 0, 1)):
     out = []
     for dg in range(-3, 4):
-        for dy in (-1, 0, 1):
+        for dy in sides:
             if (dg, dy) == (0, 0) or 2 * abs(dg) - 1 > reach:
                 continue
             if abs(dg) == 3:
@@ -283,44 +306,58 @@
     return out
 
 
+def middle_corners(wire, ref):
+    return [
+        wire.copy(ref.at[:, :, pl.ds(16, 8), :], ref.at[:, :, pl.ds(0, 8), :], 0, 1),
+        wire.copy(ref.at[:, :, pl.ds(8, 8), :], ref.at[:, :, pl.ds(24, 8), :], 0, -1),
+    ]
+
+
 class Gather:
     def __init__(self, wire, src, dst):
         self.wire, self.src, self.dst = wire, src, dst
         self.first = wire.used
         self.n = wire.ng
-        wire.used += self.n - 1
+        wire.used += self.n
         self.rows = pl.ds(16, 8)
-        self.along = []
+        self.along, self.landed = [], False
 
     def hop(self, d, plane):
         wire = self.wire
         return pltpu.make_async_remote_copy(
             src_ref=self.src,
-            dst_ref=self.dst.at[PAD2 + plane, self.rows, :],
-            send_sem=wire.send.at[self.first + d - 1],
-            recv_sem=wire.recv.at[self.first + d - 1],
+            dst_ref=self.dst.at[plane, self.rows, :],
+            send_sem=wire.send.at[self.first + d],
+            recv_sem=wire.recv.at[self.first + plane],
             device_id=((wire.g + d) % self.n, wire.y),
             device_id_type=MESH,
         )
 
     def start(self):
+        self.wire.gathers.append(self)
         for d in range(1, self.n):
             self.hop(d, self.wire.g).start()
 
     def forward(self):
-        for d in range(1, self.n):
-            self.hop(d, (self.wire.g + self.n - d) % self.n).wait_recv()
-        for dy in (-1, 1, -2, 2):
-            span = pl.ds(PAD2, self.n)
-            self.along.append(
-                self.wire.copy(
+        wire, n = self.wire, self.n
+        self.landed = True
+        groups = n // 4
+        for k in sorted(range(groups), key=lambda k: min(k, groups - k)):
+            base = 4 * ((wire.g // 4 + k) % groups)
+            for i in range(4):
+                pl.when(base + i != wire.g)(self.hop(1, base + i).wait_recv)
+            span = pl.ds(base, 4)
+            made = [
+                wire.copy(
                     self.dst.at[span, self.rows, :],
                     self.dst.at[span, pl.ds(16 - 8 * dy, 8), :],
                     0,
                     dy,
                 )
-            )
-        self.wire.start(self.along)
+                for dy in (-2, 2, -1, 1)
+            ]
+            wire.start(made)
+            self.along += made
 
     def finish(self):
         self.wire.arrive(self.along)
@@ -328,7 +365,6 @@
     def sent(self):
         for d in range(1, self.n):
             self.hop(d, self.wire.g).wait_send()
-        self.wire.sent(self.along)
 
 
 def kernel(
@@ -337,16 +373,47 @@
     in_phase, in_guess, in_rhs, rows_a, rows_b, rows_c,
     v0, s0, m0, cx0, cy0, cz0, cyl0, czl0, d0, inv0,
     v1, s1, m1, cx1, cy1, cz1, cyl1, czl1, d1, inv1,
-    v2, s2, m2, cx2, cy2, cz2, cyl2, czl2, inv2,
+    v2, s2, m2, cx2, cy2, cz2, cyl2, czl2, d2, inv2,
     send_m1, send_s1, send_e1, wide_m1, wide_s1, wide_e1,
-    send_m2, send_s2, wide_m2, wide_s2, rows_e2, rows_eb,
+    send_m2, send_s2, rows_s2, wide_m2, wide_s2, rows_e2, rows_eb,
     got_low, got_high, last_low, last_high, far_low, far_high,
     rows_p, rows_far, p_vm, r_vm,
     local, out_sem, send, recv,
 ):
     wire = Wire(ng, ny, send, recv)
+    for _ in stages(
+        wire, ng,
+    rhs, phase, guess, p_out, r_out,
+    in_phase, in_guess, in_rhs, rows_a, rows_b, rows_c,
+    v0, s0, m0, cx0, cy0, cz0, cyl0, czl0, d0, inv0,
+    v1, s1, m1, cx1, cy1, cz1, cyl1, czl1, d1, inv1,
+    v2, s2, m2, cx2, cy2, cz2, cyl2, czl2, d2, inv2,
+    send_m1, send_s1, send_e1, wide_m1, wide_s1, wide_e1,
+    send_m2, send_s2, rows_s2, wide_m2, wide_s2, rows_e2, rows_eb,
+    got_low, got_high, last_low, last_high, far_low, far_high,
+    rows_p, rows_far, p_vm, r_vm,
+    local, out_sem,
+    ):
+        pass
+    wire.drain()
+
+
+def stages(
+    wire, ng,
+    rhs, phase, guess, p_out, r_out,
+    in_phase, in_guess, in_rhs, rows_a, rows_b, rows_c,
+    v0, s0, m0, cx0, cy0, cz0, cyl0, czl0, d0, inv0,
+    v1, s1, m1, cx1, cy1, cz1, cyl1, czl1, d1, inv1,
+    v2, s2, m2, cx2, cy2, cz2, cyl2, czl2, d2, inv2,
+    send_m1, send_s1, send_e1, wide_m1, wide_s1, wide_e1,
+    send_m2, send_s2, rows_s2, wide_m2, wide_s2, rows_e2, rows_eb,
+    got_low, got_high, last_low, last_high, far_low, far_high,
+    rows_p, rows_far, p_vm, r_vm,
+    local, out_sem,
+):
     g, y = wire.g, wire.y
     fine = Level(6, 2, (v0, s0, m0, cx0, cy0, cz0, cyl0, czl0, d0, inv0), face_fine)
+    low = Level(4, 1, (v2, s2, m2, cx2, cy2, cz2, cyl2, czl2, d2, inv2), face_coarse, LANES // 2)
     mid = Level(4, 1, (v1, s1, m1, cx1, cy1, cz1, cyl1, czl1, d1, inv1), face_coarse)
 
     own = (pl.ds(3, 4), pl.ds(8, 32))
@@ -358,7 +425,7 @@
         load.start()
 
     barrier = pltpu.get_barrier_semaphore()
-    peers = [(dg, dy) for dg in range(-3, 4) for dy in (-1, 0, 1) if dy != 0 or dg == 0]
+    peers = [(dg, dy) for dg in range(-2, 3) for dy in (-1, 0, 1) if dy != 0 or dg == 0]
     peers = [p for p in peers if p != (0, 0)] + [(0, -2), (0, 2)]
     count = jnp.int32(ng - 1)
     for dg, dy in peers:
@@ -373,13 +440,14 @@
         pl.semaphore_signal(barrier, inc=1, device_id=((g + d) % ng, y), device_id_type=MESH)
     pl.semaphore_wait(barrier, count)
 
-    side = [d for d in NEAR if d[0] != 0]
-    phase_first = fine_blocks(wire, phase, in_phase, 0, 2, NEAR)
-    guess_first = fine_blocks(wire, guess, in_guess, 0, 2, NEAR)
-    rhs_first = fine_blocks(wire, rhs, in_rhs, 0, 1, NEAR)
-    phase_more = fine_blocks(wire, phase, in_phase, 2, 3, side)
-    rhs_more = fine_blocks(wire, rhs, in_rhs, 1, 2, side)
-    for group in (phase_first, guess_first, rhs_first, phase_more, rhs_more):
+    yield
+    phase_rims, guess_rims, rhs_rims = [
+        fine_rims(wire, src, dst)
+        for src, dst in ((phase, in_phase), (guess, in_guess), (rhs, in_rhs))
+    ]
+    phase_first = fine_planes(wire, phase, in_phase, 0, 2)
+    phase_more = fine_planes(wire, phase, in_phase, 2, 3)
+    for group in (phase_first, guess_rims, rhs_rims, phase_rims, phase_more):
         wire.start(group)
 
     def unpack(src, dst, low, high, first, count):
@@ -418,6 +486,36 @@
 
         planes(low, high, body)
 
+    yield
+    loads[1].wait()
+    wire.arrive(guess_rims)
+    unpack(in_guess, rows_b, 3, 7, 0, 48)
+    dense(v0, rows_b, 3, 7, (1,))
+    guess_first = [
+        wire.copy(v0.at[1, pl.ds(5, 2)], v0.at[1, pl.ds(1, 2)], 1, 0),
+        wire.copy(v0.at[1, pl.ds(3, 2)], v0.at[1, pl.ds(7, 2)], -1, 0),
+    ]
+    wire.start(guess_first)
+    loads[2].wait()
+    wire.arrive(rhs_rims)
+    unpack(in_rhs, rows_c, 3, 7, 0, 48)
+    dense(s0, rows_c, 3, 7, (0, 1))
+    rhs_first = [
+        wire.copy(s0.at[0, 6], s0.at[0, 2], 1, 0),
+        wire.copy(s0.at[0, 3], s0.at[0, 7], -1, 0),
+    ]
+    rhs_more = [
+        wire.copy(s0.at[1, 6], s0.at[1, 2], 1, 0),
+        wire.copy(s0.at[1, 3], s0.at[1, 7], -1, 0),
+        wire.copy(s0.at[0, 5], s0.at[0, 1], 1, 0),
+        wire.copy(s0.at[0, 4], s0.at[0, 8], -1, 0),
+    ]
+    wire.start(rhs_first)
+    wire.start(rhs_more)
+
+    lane = lanes_of((SUB, LANES))
+    left = lane < LANES // 2
+    pack = jnp.where(left, 2 * lane, 2 * lane - (LANES - 1))
     loads[0].wait()
     unpack_phase(3, 7, 8, 32)
     coarsest = None
@@ -433,43 +531,43 @@
                 total = 0.125 * total
                 send_m1[big, q, pl.ds(8 + half, SUB, stride=2), :] = total
                 coarsest = total if coarsest is None else coarsest + total
-    coarsest = 0.125 * coarsest
+    coarsest = jnp.take_along_axis(0.125 * coarsest, pack, axis=1)
     send_m2[...] = coarsest
-    wide_m2[PAD2 + g, pl.ds(16, 8), :] = coarsest
+    m1_blocks = middle_blocks(wire, send_m1, wide_m1, 5, (0,))
+    wire.start(m1_blocks)
+    m2_all = Gather(wire, send_m2, wide_m2)
+    m2_all.start()
+    wide_m2[g, pl.ds(16, 8), :] = coarsest
     wide_m1[pl.ds(5, 2), :, pl.ds(8, 16), :] = send_m1[:, :, pl.ds(8, 16), :]
-
-    loads[1].wait()
-    unpack(in_guess, rows_b, 3, 7, 8, 32)
-    loads[2].wait()
-    unpack(in_rhs, rows_c, 3, 7, 8, 32)
-
-    wire.arrive(phase_first, -1)
-    for x in range(1, 9):
-        if 3 <= x < 7:
-            continue
-        unpack_phase(x, x + 1, 0, 48)
+    wire.arrive(phase_rims, -1)
     unpack_phase(3, 7, 0, 8)
     unpack_phase(3, 7, 40, 8)
+
+    wire.arrive(phase_first, -1)
+    corners_first = fine_corners(wire, in_phase, ((1, 2), (7, 2)))
+    wire.start(corners_first)
+    unpack_phase(1, 3, 8, 32)
+    unpack_phase(7, 9, 8, 32)
+    wire.arrive(phase_more, -1)
+    corners_more = fine_corners(wire, in_phase, ((0, 1), (9, 1)))
+    wire.start(corners_more)
+    yield
+    wire.arrive(corners_first, -1)
+    for first in (0, 40):
+        unpack_phase(1, 3, first, 8)
+        unpack_phase(7, 9, first, 8)
     dense(m0, rows_a, 1, 9, (0, 1))
     fine.faces_x(1, 8)
     fine.faces_yz(2, 8)
     fine.diagonals(2, 8)
-
+    yield
     wire.arrive(guess_first)
-    unpack(in_guess, rows_b, 1, 3, 0, 48)
-    unpack(in_guess, rows_b, 7, 9, 0, 48)
-    unpack(in_guess, rows_b, 3, 7, 0, 8)
-    unpack(in_guess, rows_b, 3, 7, 40, 8)
-    dense(v0, rows_b, 1, 9, (1,))
     wire.arrive(rhs_first)
-    unpack(in_rhs, rows_c, 2, 3, 0, 48)
-    unpack(in_rhs, rows_c, 7, 8, 0, 48)
-    unpack(in_rhs, rows_c, 3, 7, 0, 8)
-    unpack(in_rhs, rows_c, 3, 7, 40, 8)
-    dense(s0, rows_c, 2, 8, (0, 1))
-
-    def sweep_one():
+    yield
+
+    def sweep_one(waiting=()):
         fine.colour_pass(0, 2, 8)
+        wire.sent(waiting)
         fine.colour_pass(1, 3, 7)
 
     def exchange(low, high):
@@ -488,14 +586,14 @@
         wire.sent(copies)
         fine.colour_pass(1, 2, 8)
 
-    sweep_one()
+    sweep_one(guess_first)
+    yield
     swap = exchange(got_low, got_high)
-    m1_blocks = middle_blocks(wire, send_m1, wide_m1, 5)
-    wire.start(m1_blocks)
-    m2_all = Gather(wire, send_m2, wide_m2)
-    m2_all.start()
-
-    wire.arrive(phase_more, -1)
+    wire.arrive(m1_blocks)
+    m1_corners = middle_corners(wire, wide_m1)
+    wire.start(m1_corners)
+    m2_all.forward()
+    wire.arrive(corners_more, -1)
     unpack_phase(0, 1, 0, 48)
     unpack_phase(9, 10, 0, 48)
     dense(m0, rows_a, 0, 1, (0, 1))
@@ -507,13 +605,10 @@
     fine.diagonals(1, 2)
     fine.diagonals(8, 9)
     wire.arrive(rhs_more)
-    unpack(in_rhs, rows_c, 1, 2, 0, 48)
-    unpack(in_rhs, rows_c, 8, 9, 0, 48)
-    dense(s0, rows_c, 1, 2, (0, 1))
-    dense(s0, rows_c, 8, 9, (0, 1))
-
+    yield
     sweep_two(swap, got_low, got_high)
 
+    yield
     for big in range(2):
         for r1 in range(3):
             total = [None, None]
@@ -529,6 +624,7 @@
     wire.start(s1_blocks)
     wide_s1[pl.ds(5, 2), :, pl.ds(8, 16), :] = send_s1[:, :, pl.ds(8, 16), :]
 
+    yield
     for x in range(3, 7):
         for c in (0, 1):
             for r in range(6):
@@ -543,7 +639,8 @@
     ]
     wire.start(far)
 
-    wire.arrive(m1_blocks)
+    yield
+    wire.arrive(m1_corners)
 
     def dense_mid(ref, rows, low, high, colours):
         def body(x, par):
@@ -557,7 +654,6 @@
     mid.faces_x(0, 11)
     mid.faces_yz(1, 11)
     mid.diagonals(1, 11)
-    m2_all.forward()
     v1[1] = jnp.zeros(v1.shape[1:], F32)
 
     def sweeps_mid():
@@ -566,7 +662,9 @@
         mid.colour_pass(0, 3, 9)
         mid.colour_pass(1, 4, 8)
 
+    yield
     wire.arrive(s1_blocks)
+    yield
     dense_mid(s1, wide_s1, 1, 11, (0, 1))
     sweeps_mid()
     for r2 in range(2):
@@ -576,98 +674,88 @@
                 for c in (0, 1):
                     part = mid.residual(c, x, x % 2, r)[0]
                     total = part if total is None else total + part
-        send_s2[pl.ds(4 + r2, SUB, stride=2), :] = 0.5 * total
-    s2_all = Gather(wire, send_s2.at[pl.ds(8, 8), :], wide_s2)
+        rows_s2[pl.ds(4 + r2, SUB, stride=2), :] = 0.5 * total
+    send_s2[...] = jnp.take_along_axis(rows_s2[pl.ds(8, 8), :], pack, axis=1)
+    yield
+    s2_all = Gather(wire, send_s2, wide_s2)
     s2_all.start()
-    wide_s2[PAD2 + g, pl.ds(16, 8), :] = send_s2[pl.ds(8, 8), :]
+    wide_s2[g, pl.ds(16, 8), :] = send_s2[...]
     for x in (5, 6):
         for c in (0, 1):
             for r in range(4):
                 b = mid.bit(c, x % 2, r)
                 send_e1[x - 5, b, pl.ds(r, SUB, stride=4), :] = v1[c, x, r, 0]
-    e1_blocks = middle_blocks(wire, send_e1, wide_e1, 5)
+    e1_blocks = middle_blocks(wire, send_e1, wide_e1, 5, (0,))
     wire.start(e1_blocks)
     wide_e1[pl.ds(5, 2), :, pl.ds(8, 16), :] = send_e1[:, :, pl.ds(8, 16), :]
 
+    yield
     m2_all.finish()
-    lane = lanes_of((SUB, LANES))
-    last = lane == LANES - 1
-    zero = jnp.zeros((SUB, LANES), F32)
+    half = ng // 2
+
+    def load_low(ref, rows):
+        def body(x, par):
+            for r in range(4):
+                at = pl.ds(4 + r, SUB, stride=4)
+                one, two = rows[x - 1, at, :], rows[x - 1 + half, at, :]
+                even = jnp.where(left, one, roll(two, LANES // 2, 1))
+                odd = jnp.where(left, roll(one, LANES // 2, 1), two)
+                for c in (0, 1):
+                    ref[c, x, r, 0] = odd if low.bit(c, par, r) else even
+
+        planes(1, half + 1, body)
+
+    load_low(m2, wide_m2)
+    for c in (0, 1):
+        for r in range(4):
+            m2[c, 0, r, 0] = jnp.where(left, 0.0, roll(m2[c, half, r, 0], LANES // 2, 1))
+            m2[c, half + 1, r, 0] = jnp.where(left, roll(m2[c, 1, r, 0], LANES // 2, 1), 0.0)
+    v2[1] = jnp.zeros(v2.shape[1:], F32)
+    low.faces_x(0, half + 1)
+    low.faces_yz(1, half + 1)
+    low.diagonals(1, half + 1)
+    yield
+    s2_all.forward()
+    wire.arrive(e1_blocks)
+    e1_corners = middle_corners(wire, wide_e1)
+    wire.start(e1_corners)
+    yield
+    s2_all.finish()
+    yield
+    load_low(s2, wide_s2)
+
+    def pass_low(c):
+        for r in range(4):
+            v2[1 - c, 0, r, 0] = roll(v2[1 - c, half, r, 0], LANES // 2, 1)
+            v2[1 - c, half + 1, r, 0] = roll(v2[1 - c, 1, r, 0], LANES // 2, 1)
+        low.colour_pass(c, 1, half + 1)
+
+    def sweep_low(i, carry):
+        pass_low(0)
+        pass_low(1)
+        return carry
+
+    lax.fori_loop(0, 4, sweep_low, 0)
+    yield
+    natural = (lane % 2) * (LANES // 2) + lane // 2
+
+    def keep_low(x, par):
+        for r in range(4):
+            parts = [v2[c, x, r, 0] for c in (0, 1)]
+            even, odd = parts if low.bit(0, par, r) == 0 else parts[::-1]
+            at = pl.ds(r, SUB, stride=4)
+            one = jnp.where(left, even, roll(odd, LANES // 2, 1))
+            two = jnp.where(left, roll(even, LANES // 2, 1), odd)
+            rows_e2[PAD2 + x - 1, at, :] = jnp.take_along_axis(one, natural, axis=1)
+            rows_e2[PAD2 + x - 1 + half, at, :] = jnp.take_along_axis(two, natural, axis=1)
+
+    planes(1, half + 1, keep_low)
     for x in range(PAD2):
-        for r in range(4):
-            for ref in (v2, m2, cx2):
-                ref[x, r] = zero
-                ref[PAD2 + ng + x, r] = zero
-
-    def load_two(ref, rows):
-        def body(x, carry):
-            for r in range(4):
-                ref[x, r] = rows[x, pl.ds(4 + r, SUB, stride=4), :]
-            return carry
-
-        lax.fori_loop(PAD2, PAD2 + ng, body, 0)
-
-    load_two(m2, wide_m2)
-
-    def faces_two(x, carry):
-        for r in range(4):
-            here = m2[x, r]
-            cx2[x, r] = face_coarse(here, m2[x + 1, r])
-            cy2[x, r] = face_coarse(here, m2[x, r + 1] if r < 3 else roll(m2[x, 0], -1, 0))
-            up = jnp.where(last, 0.0, face_coarse(here, roll(here, -1, 1)))
-            cz2[x, r] = up
-            czl2[x, r] = roll(up, 1, 1)
-        cyl2[x] = roll(cy2[x, 3], 1, 0)
-        for r in range(4):
-            yl = cy2[x, r - 1] if r else cyl2[x]
-            total = cx2[x - 1, r] + cx2[x, r] + yl + cy2[x, r] + cz2[x, r] + czl2[x, r]
-            total = total + jnp.where(last, 2.0 * m2[x, r], 0.0)
-            inv2[x, r] = 1.0 / jnp.where(total > 0, total, 1.0)
-            v2[x, r] = zero
-        return carry
-
-    lax.fori_loop(PAD2, PAD2 + ng, faces_two, 0)
-
-    s2_all.forward()
-    s2_all.finish()
-    load_two(s2, wide_s2)
-
-    def pass_two(c):
-        def one(x, par):
-            field = [v2[x, r] for r in range(4)]
-            below, above = roll(field[3], 1, 0), roll(field[0], -1, 0)
-            for r in range(4):
-                yl = field[r - 1] if r else below
-                yu = field[r + 1] if r < 3 else above
-                total = cx2[x - 1, r] * v2[x - 1, r] + cx2[x, r] * v2[x + 1, r]
-                total = total + ((cy2[x, r - 1] if r else cyl2[x]) * yl + cy2[x, r] * yu)
-                total = total + (czl2[x, r] * roll(field[r], 1, 1) + cz2[x, r] * roll(field[r], -1, 1))
-                value = (s2[x, r] + total) * inv2[x, r]
-                hit = (lane + (par + r + c)) % 2 == 0
-                v2[x, r] = jnp.where(hit, value, field[r])
-
-        def pair(i, carry):
-            one(PAD2 + 2 * i, 0)
-            one(PAD2 + 2 * i + 1, 1)
-            return carry
-
-        lax.fori_loop(0, ng // 2, pair, 0)
-
-    def sweep_of_two(i, carry):
-        pass_two(0)
-        pass_two(1)
-        return carry
-
-    lax.fori_loop(0, 4, sweep_of_two, 0)
-
-    def keep_two(x, carry):
-        for r in range(4):
-            rows_e2[x, pl.ds(r, SUB, stride=4), :] = v2[x, r]
-        return carry
-
-    lax.fori_loop(0, ng + 2 * PAD2, keep_two, 0)
-
-    wire.arrive(e1_blocks)
+        rows_e2[x] = jnp.zeros((32, LANES), F32)
+        rows_e2[PAD2 + ng + x] = jnp.zeros((32, LANES), F32)
+
+    yield
+    wire.arrive(e1_corners)
     for x in range(12):
         source = g + ((x + 1) // 2 - 3 + PAD2)
         for r in range(4):
@@ -680,6 +768,7 @@
                 b = mid.bit(c, x % 2, r)
                 rows_eb[x - 4, b, pl.ds(r, SUB, stride=4), :] = v1[c, x, r, 0]
 
+    yield
     wire.arrive(far[2:])
     wire.arrive(far[:2])
     wire.sent(far)
@@ -696,10 +785,13 @@
             for j in range(2):
                 add = rows_eb[(x - 1) // 2, j, pl.ds(4 + r // 2, SUB, stride=3), :]
                 v0[1, x, r, j] = v0[1, x, r, j] + add
+    yield
     sweep_one()
     swap_last = exchange(last_low, last_high)
+    yield
     sweep_two(swap_last, last_low, last_high)
 
+    yield
     for x in range(3, 7):
         for c in (0, 1):
             for r in range(6):
@@ -719,10 +811,6 @@
     ]
     for out in outs:
         out.start()
-    for group in (phase_first, guess_first, rhs_first, phase_more, rhs_more, m1_blocks, s1_blocks, e1_blocks):
-        wire.sent(group)
-    m2_all.sent()
-    s2_all.sent()
     for out in outs:
         out.wait()
 
@@ -733,11 +821,10 @@
     two = ng + 2 * PAD2
     shapes = [pltpu.VMEM((10, 48, 512), jnp.int32), pltpu.VMEM((10, 48, 512), F32), pltpu.VMEM((10, 48, 512), F32)]
     shapes += [rows(10, 4, 48)] * 3
-    for n, r, j in ((10, 6, 2), (12, 4, 1)):
+    for n, r, j in ((10, 6, 2), (12, 4, 1), (ng // 2 + 2, 4, 1)):
         shapes += [vec(2, n, r, j)] * 6 + [vec(2, n, j), vec(2, n, r)] + [vec(2, n, r, j)] * 2
-    shapes += [vec(two, 4)] * 6 + [vec(two)] + [vec(two, 4)] * 2
     shapes += [rows(2, 2, 32)] * 3 + [rows(12, 2, 32)] * 3
-    shapes += [rows(8), rows(24), rows(two, 40), rows(two, 40), rows(two, 32), rows(4, 2, 32)]
+    shapes += [rows(8), rows(8), rows(24), rows(ng, 40), rows(ng, 40), rows(two, 32), rows(4, 2, 32)]
     shapes += [vec(3, 6, 2)] * 4 + [vec(1, 6, 2)] * 2
     shapes += [rows(4, 4, 48)] * 2 + [pltpu.VMEM((4, 32, 512), F32), pltpu.VMEM((4, 32, 512), F32)]
     count = 160

time: 72.4 us -> 63.6 us (0.88)
  Pallas kernels: 69.2 us -> 60.4 us
    pallas_call x1, Pallas kernels: 69.2 us -> 60.4 us  [local(): pl.pallas_call(functools.partial(kernel, ng, ny), out_shape=(out, out), i...]
where the time goes in v2:
time: 63.6 us; the launch traced here: 63.4 us
  Pallas kernels  60.4 us (95%)
  local copies, waits for them, and re-layouts  2.42 us (4%)
  between operations  0.65 us (1%)
    pallas_call x1, Pallas kernels, local(): pl.pallas_call(functools.partial(kernel, ng, ny), out_shape=(out, out), i...  60.4 us
    unnamed x4, local copies, waits for them, and re-layouts  2.42 us

profile of v2, /device:TPU:8, one launch (start us, length us, event | category | flops | bytes accessed | tf_op | source)
XLA Modules:
  0.0 63.4 jit_solution(14539732502794138160)
XLA Ops:
  0.6 60.4 %vcycle.1 = (f32[4,32,512]{2,1,0:T(8,128)}, f32[4,32,512]{2,1,0:T(8,128)}) custom-call(f32[4,32,512]{2,1,0:T(8,128)} %rhs.1, s32[4,32,512]{2,1,0:T(8,128)} %phase.1, f32[4,32,512]{2,1,0:T(8,128)} %guess.1), custom_call_target="tpu_custom_call" | custom-call | tf_op jit(solution)/shard_map/vcycle/pallas_call | solution.py:842
  61.0 0.0 copy-start
  61.0 1.7 %copy.7 = f32[4,32,512]{2,1,0:T(8,128)} copy(f32[4,32,512]{2,1,0:T(8,128)} %get-tuple-element.4) | data formatting | bytes 524288
  62.7 0.0 copy-done
  62.7 0.7 %copy.8 = f32[4,32,512]{2,1,0:T(8,128)} copy(f32[4,32,512]{2,1,0:T(8,128)S(1)} %copy-done) | data formatting | bytes 524288
Async XLA Ops:
  61.0 1.7 %copy-start = (f32[4,32,512]{2,1,0:T(8,128)S(1)}, f32[4,32,512]{2,1,0:T(8,128)}, u32[]{:S(2)}) copy-start(f32[4,32,512]{2,1,0:T(8,128)} %get-tuple-element.5) | copy-start | bytes 786436
